TPU v7x, 32 devices: a whole 2x2x4 slice. The times are simulated.
32 devices in a mesh: groups: 2 (over x), seq: 4 (over y, core), head: 4 (over z).
Axes of the slice: x: 2, y: 2, z: 4, core: 2. Of those that a mesh axis runs over, the one named last changes fastest.
Arguments:
- patches: bfloat16 [32768, 1024], P(('groups', 'seq')), parts along dimension 0, may hold values from -100 to 100, as said below
- w_qkv: bfloat16 [1024, 3, 1024], P(None, None, 'head'), may hold values from -0.1875 to 0.1875
Outputs:
- mixed: bfloat16 [32768, 1024], P(('groups', 'seq'), 'head'), parts along dimension 0
There are 2 independent parts, one for each index of `groups`. A program takes and returns all parts, laid end to end along the dimension named above; an argument that names none is the same for every part. Nothing has to cross between parts.
Inputs may be any that keep to these rules, and one draw needn't show every extreme that they name: `patches`: entries are finite.
All inputs are finite; a program needn't handle non-finite values.
Results may differ from a plain program's by a relative error of at most 0.0012.
The roundings to bfloat16 on the way count: a program that leaves them out, or rounds other values in their place, can miss the bound.
Values may be sent and summed in bfloat16 or wider, within the bound.
No kernel may reach another device: no remote copies, remote signals or barrier semaphores. Data moves between devices by JAX's collectives and lax.ppermute only.
A program may use at most 192 MiB of HBM per device.

v0:
```python
import functools
import math

import jax
import jax.numpy as jnp
from jax import lax
from jax.experimental import pallas as pl
from jax.experimental.pallas import tpu as pltpu
from jax.sharding import PartitionSpec as P

D = 1024
HEAD_DIM = 64
COLS = 256
NEG_BIG = -1e30

STRIP = 16
BOTH = 2 * STRIP
PACK = 4

F32 = jnp.float32
BF16 = jnp.bfloat16


def shifted(block, axis, distance):
    devices = range(lax.axis_size(axis))
    route = [(i - distance, i) for i in devices if i - distance in devices]
    return lax.ppermute(block, axis, route)


def row_attention(queries, key_rows, value_rows, prev_keys, prev_values, first_row):
    row_count = queries.shape[1]
    scale = 1.0 / math.sqrt(HEAD_DIM)
    earlier_keys = jnp.concatenate([prev_keys[:, None], key_rows[:, :-1]], 1)
    earlier_values = jnp.concatenate([prev_values[:, None], value_rows[:, :-1]], 1)
    score_prev = (
        jnp.einsum("hrce,hrje->hrcj", queries, earlier_keys, preferred_element_type=jnp.float32)
        * scale
    )
    score_own = (
        jnp.einsum("hrce,hrje->hrcj", queries, key_rows, preferred_element_type=jnp.float32) * scale
    )
    column = lax.broadcasted_iota(jnp.int32, (1, 1, COLS, COLS), 2)
    slot = lax.broadcasted_iota(jnp.int32, (1, 1, COLS, COLS), 3)
    row_index = lax.broadcasted_iota(jnp.int32, (1, row_count, 1, 1), 1) + first_row
    allowed_prev = (slot > column) & (row_index > 0)
    allowed_own = slot <= column
    score_prev = jnp.where(allowed_prev, score_prev, NEG_BIG)
    score_own = jnp.where(allowed_own, score_own, NEG_BIG)
    highest = jnp.maximum(
        jnp.max(score_prev, axis=-1, keepdims=True), jnp.max(score_own, axis=-1, keepdims=True)
    )
    terms_prev = jnp.where(allowed_prev, jnp.exp(score_prev - highest), 0.0)
    terms_own = jnp.where(allowed_own, jnp.exp(score_own - highest), 0.0)
    totals = jnp.sum(terms_prev, axis=-1, keepdims=True) + jnp.sum(
        terms_own, axis=-1, keepdims=True
    )
    context = jnp.einsum(
        "hrcj,hrje->hrce",
        terms_prev.astype(jnp.bfloat16),
        earlier_values,
        preferred_element_type=jnp.float32,
    )
    context = context + jnp.einsum(
        "hrcj,hrje->hrce",
        terms_own.astype(jnp.bfloat16),
        value_rows,
        preferred_element_type=jnp.float32,
    )
    return context / totals


def column_attention(queries, key_rows, value_rows):
    row_count = queries.shape[1]
    scores = jnp.einsum(
        "hrce,hsce->hcrs", queries, key_rows, preferred_element_type=jnp.float32
    ) * (1.0 / math.sqrt(HEAD_DIM))
    later = lax.broadcasted_iota(jnp.int32, (1, 1, row_count, row_count), 2)
    earlier = lax.broadcasted_iota(jnp.int32, (1, 1, row_count, row_count), 3)
    allowed = earlier <= later
    scores = jnp.where(allowed, scores, NEG_BIG)
    highest = jnp.max(scores, axis=-1, keepdims=True)
    terms = jnp.where(allowed, jnp.exp(scores - highest), 0.0)
    totals = jnp.sum(terms, axis=-1, keepdims=True)
    context = jnp.einsum(
        "hcrs,hsce->hcre",
        terms.astype(jnp.bfloat16),
        value_rows,
        preferred_element_type=jnp.float32,
    )
    return jnp.transpose((context / totals).astype(jnp.bfloat16), (0, 2, 1, 3))


def general(patches, w_qkv):
    local_width = w_qkv.shape[2]
    head_count = local_width // HEAD_DIM
    row_count = patches.shape[0] // COLS
    weights_heads = w_qkv.reshape(D, 3, head_count, HEAD_DIM)
    projected = jnp.einsum(
        "td,dkhe->khte", patches, weights_heads, preferred_element_type=jnp.float32
    ).astype(jnp.bfloat16)
    prev_inputs = shifted(patches[-COLS:], "seq", 1)
    prev_pair = jnp.einsum(
        "td,dkhe->khte", prev_inputs, weights_heads[:, 1:], preferred_element_type=jnp.float32
    ).astype(jnp.bfloat16)
    first_row = lax.axis_index("seq") * row_count
    stacked = projected.reshape(3, head_count, row_count, COLS, HEAD_DIM)
    row_context = row_attention(
        stacked[0], stacked[1], stacked[2], prev_pair[0], prev_pair[1], first_row
    )
    column_pack = lax.all_to_all(stacked, "seq", split_axis=3, concat_axis=2, tiled=True)
    column_context = column_attention(column_pack[0], column_pack[1], column_pack[2])
    returned = lax.all_to_all(column_context, "seq", split_axis=1, concat_axis=2, tiled=True)
    mixed = (0.5 * (row_context + returned.astype(jnp.float32))).astype(jnp.bfloat16)
    return jnp.transpose(mixed, (1, 2, 0, 3)).reshape(row_count * COLS, local_width)


def iota(shape, axis):
    return lax.broadcasted_iota(jnp.int32, shape, axis)


def dot(left, right):
    return jnp.dot(left, right, preferred_element_type=F32)


def dot_t(left, right):
    return lax.dot_general(left, right, (((1,), (1,)), ((), ())), preferred_element_type=F32)


SLICES = 3
HALF = COLS // 2
ANYWHERE = pl.BlockSpec(memory_space=pl.ANY)
ON_CHIP = pl.BlockSpec(memory_space=pltpu.VMEM)


def call(kernel, info, operands, out_shape, scratch=(), **more):
    options = dict(
        in_specs=[ON_CHIP] * len(operands),
        out_specs=jax.tree.map(lambda _: ON_CHIP, out_shape),
    )
    aliases = more.pop("aliases", {})
    name = more.pop("name")
    flops = more.pop("flops", 1)
    options.update(more)
    return pl.pallas_call(
        kernel,
        out_shape=out_shape,
        grid_spec=pltpu.PrefetchScalarGridSpec(
            num_scalar_prefetch=1,
            grid=options.pop("grid", ()),
            scratch_shapes=list(scratch),
            **options,
        ),
        input_output_aliases=aliases,
        compiler_params=pltpu.CompilerParams(vmem_limit_bytes=28 << 20),
        cost_estimate=pl.CostEstimate(flops=flops, bytes_accessed=1, transcendentals=0),
        name=name,
    )(info, *operands)


def column_span(info, other, first, cols):
    half = 1 - info[0] if other else info[0]
    return pl.ds(pl.multiple_of(half * HALF + first, 16), cols)


def sent_slot(info):
    return jnp.where(info[1] == 0, 2, 0)


def projected(x, w, natural_ref, last_ref, turned_refs, slot, columns, rows):
    _, block, depth = x.shape
    part = STRIP // 2
    parts = [
        dot(x[r : r + part].reshape(part * block, depth), w).astype(BF16) for r in (0, part)
    ]
    value = jnp.concatenate(parts, 0).reshape(STRIP, block, w.shape[1])
    natural_ref[slot, :, columns, :] = value

    @pl.when(slot > 0)
    def _():
        last_ref[slot - 1, columns, :] = value[STRIP - 1]

    turned = jnp.swapaxes(value, 0, 1)
    for ref in turned_refs:
        ref[rows] = turned


def first_kernel(info, x_ref, w_ref, *refs, block):
    natural_ref, mine_ref, other_ref, last_ref, send_mine_ref, send_other_ref, x_out = refs[:7]
    w_buf, x_sem, w_sem = refs[7:]
    slot = sent_slot(info)
    w_copy = pltpu.make_async_copy(w_ref.at[slot], w_buf, w_sem)
    w_copy.start()
    pieces = []
    for other in (False, True):
        for first in range(0, HALF, block):
            columns = column_span(info, other, first, block)
            copy = pltpu.make_async_copy(
                x_ref.at[:, columns, :], x_out.at[:, columns, :], x_sem.at[len(pieces)]
            )
            copy.start()
            pieces.append((copy, other, first, columns))
    w_copy.wait()
    w = w_buf[...]
    for copy, other, first, columns in pieces:
        copy.wait()
        triple_ref = other_ref if other else mine_ref
        send_ref = send_other_ref if other else send_mine_ref
        projected(
            x_out[:, columns, :],
            w,
            natural_ref,
            last_ref,
            (triple_ref.at[slot], send_ref),
            slot,
            columns,
            pl.ds(first, block),
        )


def rest_kernel(info, x_ref, w_ref, *refs, block):
    natural_ref, mine_ref, other_ref, last_ref = refs[-4:]
    for slot in (2 - sent_slot(info), 1):
        w = w_ref[slot]
        for other, triple_ref in ((False, mine_ref), (True, other_ref)):
            for first in range(0, HALF, block):
                columns = column_span(info, other, first, block)
                projected(
                    x_ref[:, columns, :],
                    w,
                    natural_ref,
                    last_ref,
                    (triple_ref.at[slot],),
                    slot,
                    columns,
                    pl.ds(first, block),
                )


def project(info, x, w, block=64):
    width = w.shape[2]
    natural = jax.ShapeDtypeStruct((3, STRIP, COLS, width), BF16)
    triple = jax.ShapeDtypeStruct((3, HALF, STRIP, width), BF16)
    last = jax.ShapeDtypeStruct((2, COLS, width), BF16)
    single = jax.ShapeDtypeStruct((HALF, STRIP, width), BF16)
    return call(
        functools.partial(first_kernel, block=block),
        info,
        [x, w],
        [natural, triple, triple, last, single, single, jax.ShapeDtypeStruct(x.shape, BF16)],
        [
            pltpu.VMEM(w.shape[1:], BF16),
            pltpu.SemaphoreType.DMA((COLS // block,)),
            pltpu.SemaphoreType.DMA,
        ],
        in_specs=[ANYWHERE] * 2,
        name="project_sent",
    )


def project_rest(info, x, w, kept, block=64):
    return call(
        functools.partial(rest_kernel, block=block),
        info,
        [x, w] + list(kept),
        [jax.ShapeDtypeStruct(array.shape, BF16) for array in kept],
        aliases={3 + n: n for n in range(len(kept))},
        name="project_rest",
    )


def heads_of(shape, axis):
    return iota(shape, axis) // HEAD_DIM


def head_rows(rows_per_head, width):
    shape = (rows_per_head * (width // HEAD_DIM), width)
    own = iota(shape, 0) // rows_per_head == iota(shape, 1) // HEAD_DIM
    return jnp.where(own, 1.0 / math.sqrt(HEAD_DIM), 0.0).astype(BF16)


def row_kernel(info, *refs, width, top, rows):
    before_k_ref, before_v_ref, q_ref, k_ref, v_ref, out_ref, prev_k, prev_v = refs
    step = pl.program_id(0)
    heads = width // HEAD_DIM

    @pl.when(step == 0)
    def _():
        prev_k[...] = before_k_ref[0] if top else before_k_ref[0, 0]
        prev_v[...] = before_v_ref[0] if top else before_v_ref[0, 0]

    own = iota((COLS, COLS), 1) <= iota((COLS, COLS), 0)
    lane_head = heads_of((COLS, width), 1)
    scale = 1.0 / math.sqrt(HEAD_DIM)
    spread = [jnp.where(lane_head == h, scale, 0.0).astype(BF16) for h in range(heads)]
    earlier_k, earlier_v = prev_k[...], prev_v[...]
    for r in range(rows):
        q, k, v = q_ref[0, r], k_ref[0, r], v_ref[0, r]
        result = None
        for h in range(heads):
            masked = q * spread[h]
            scores_prev = dot_t(masked, earlier_k)
            if top and r == 0:
                first = (step == 0) & (info[2] == 0)
                scores_prev = scores_prev + jnp.where(first, NEG_BIG, 0.0)
            scores = jnp.where(own, dot_t(masked, k), scores_prev)
            terms = jnp.exp(scores - jnp.max(scores, axis=1, keepdims=True))
            inverse = 1.0 / jnp.sum(terms, axis=1, keepdims=True)
            context = dot(jnp.where(own, terms, 0.0).astype(BF16), v)
            context = context + dot(jnp.where(own, 0.0, terms).astype(BF16), earlier_v)
            context = context * inverse
            result = context if h == 0 else jnp.where(lane_head == h, context, result)
        out_ref[r] = result
        earlier_k, earlier_v = k, v
    prev_k[...] = earlier_k
    prev_v[...] = earlier_v


def row_part(info, halo, natural, first_row, row_count, rows=4):
    width = natural.shape[3]
    top = first_row == 0
    block = (1, rows, COLS, width)

    def spec(slot):
        return pl.BlockSpec(block, lambda r, info: (slot, first_row // rows + r, 0, 0))

    def before_spec(slot):
        if top:
            return pl.BlockSpec((1, COLS, width), lambda r, info: (slot - 1, 0, 0))
        return pl.BlockSpec((1, 1, COLS, width), lambda r, info: (slot, first_row - 1, 0, 0))

    return call(
        functools.partial(row_kernel, width=width, top=top, rows=rows),
        info,
        [halo if top else natural] * 2 + [natural] * 3,
        jax.ShapeDtypeStruct((row_count, COLS, width), F32),
        [pltpu.VMEM((COLS, width), BF16)] * 2,
        grid=(row_count // rows,),
        in_specs=[before_spec(1), before_spec(2)] + [spec(slot) for slot in range(3)],
        out_specs=pl.BlockSpec((rows, COLS, width), lambda r, info: (r, 0, 0)),
        flops=2 * 10**10,
        name="row_attention",
    )


def column_of(mine, other, j):
    return jnp.concatenate([mine[j], other[j]], 0)


def scores_of(keys, queries, spread, heads):
    return dot_t(keys, jnp.concatenate([queries] * heads, 0) * spread)


def later_key(core, heads):
    shape = (BOTH, heads * BOTH)
    key_row = (iota(shape, 0) + STRIP * core) & (BOTH - 1)
    query_row = (iota(shape, 1) + STRIP * core) & (BOTH - 1)
    return key_row > query_row


def by_pack(first, count, body):
    def run(g, carry):
        body(g, pl.ds(first + g * PACK, PACK))
        return carry

    lax.fori_loop(0, count // PACK, run, 0, unroll=4)


def maxima_kernel(info, mine_ref, other_ref, out_ref, *, heads):
    hidden = later_key(info[0], heads)
    spread = head_rows(BOTH, heads * HEAD_DIM)

    def body(g, part):
        qm, qo = mine_ref[0, part], other_ref[0, part]
        km, ko = mine_ref[1, part], other_ref[1, part]
        tops = []
        for j in range(PACK):
            scores = scores_of(column_of(km, ko, j), column_of(qm, qo, j), spread, heads)
            tops.append(jnp.max(jnp.where(hidden, NEG_BIG, scores), axis=0, keepdims=True))
        out_ref[part] = jnp.concatenate(tops, 0)

    @pl.when(info[1] == 1)
    def _():
        by_pack(0, mine_ref.shape[1], body)


def maxima(info, mine, other):
    heads = mine.shape[-1] // HEAD_DIM
    return call(
        functools.partial(maxima_kernel, heads=heads),
        info,
        [mine, other],
        jax.ShapeDtypeStruct((mine.shape[1], heads * BOTH), F32),
        name="maxima",
    )


def weights_kernel(
    info, qm_ref, qo_ref, mine_ref, other_ref, top_ref, w_ref, stats, *, heads, first, cols
):
    spread = head_rows(BOTH, heads * HEAD_DIM)

    def body(g, part):
        qm, qo = qm_ref[part], qo_ref[part]
        km, ko = mine_ref[1, part], other_ref[1, part]
        below = top_ref[part]
        tops, totals, turned = [], [], []
        for j in range(PACK):
            scores = scores_of(column_of(km, ko, j), column_of(qm, qo, j), spread, heads)
            top = jnp.maximum(jnp.max(scores, axis=0, keepdims=True), below[j : j + 1])
            terms = jnp.exp(scores - top)
            tops.append(top)
            totals.append(jnp.sum(terms, axis=0, keepdims=True))
            turned.append(terms)
        w_ref[pl.ds(g * heads * BOTH, heads * BOTH)] = jnp.concatenate(turned, 0).T.astype(BF16)
        stats[0, pl.ds(g * PACK, PACK)] = jnp.concatenate(tops, 0)
        stats[1, pl.ds(g * PACK, PACK)] = jnp.concatenate(totals, 0)

    @pl.when(info[1] == 0)
    def _():
        by_pack(first, cols, body)
        rest = stats[...].reshape(2 * cols, heads * BOTH)
        at = cols // PACK * heads * BOTH
        for n in range(SLICES):
            part = rest.astype(BF16)
            w_ref[at + n * 2 * cols : at + (n + 1) * 2 * cols] = part
            rest = rest - part.astype(F32)


def cross_weights(info, recv_mine, recv_other, mine, other, top, first, cols):
    heads = mine.shape[-1] // HEAD_DIM
    rows = heads * BOTH
    return call(
        functools.partial(weights_kernel, heads=heads, first=first, cols=cols),
        info,
        [recv_mine, recv_other, mine, other, top],
        jax.ShapeDtypeStruct((cols // PACK * rows + SLICES * 2 * cols, PACK * BOTH), BF16),
        [pltpu.VMEM((2, cols, rows), F32)],
        name="cross_weights",
    )


def column_kernel(
    info, mine_ref, other_ref, vm_ref, vo_ref, w_ref, om_ref, oo_ref, stats, *, heads, first, cols
):
    hidden = later_key(info[0], heads)
    width = heads * HEAD_DIM
    rows = heads * BOTH
    spread = head_rows(BOTH, width)
    lower = info[1] == 1
    pair = 2 * BOTH
    keys = PACK * BOTH
    key_column = (iota((1, 2 * keys), 1) & (keys - 1)) // BOTH
    picks = [jnp.where(key_column == j, 1.0, 0.0).astype(BF16) for j in range(PACK)]
    left_head = iota((BOTH, 2 * HEAD_DIM), 1) < HEAD_DIM
    at = cols // PACK * rows
    whole = w_ref[at : at + 2 * cols].astype(F32)
    for n in range(1, SLICES):
        whole = whole + w_ref[at + n * 2 * cols : at + (n + 1) * 2 * cols].astype(F32)
    stats[...] = whole.reshape(stats.shape)

    def body(g, part):
        local = pl.ds(g * PACK, PACK)
        qm, qo = mine_ref[0, part], other_ref[0, part]
        km, ko = mine_ref[1, part], other_ref[1, part]
        above, far_totals = stats[0, local], stats[1, local]
        totals, turned = [], []
        for j in range(PACK):
            scores = scores_of(column_of(km, ko, j), column_of(qm, qo, j), spread, heads)
            scores = jnp.where(hidden, NEG_BIG, scores)
            top = jnp.max(scores, axis=0, keepdims=True)
            top = jnp.where(lower, above[j : j + 1], top)
            terms = jnp.exp(scores - top)
            totals.append(jnp.sum(terms, axis=0, keepdims=True))
            turned.append(terms)
        inverse = 1.0 / (jnp.concatenate(totals, 0) + far_totals)
        inverse = jnp.concatenate([inverse, inverse], 0).T
        near = jnp.concatenate(turned, 0).T.astype(BF16)
        weights = jnp.concatenate([near, w_ref[pl.ds(g * rows, rows)]], 1)
        near_v = [column_of(mine_ref[2, part], other_ref[2, part], j) for j in range(PACK)]
        far_v = [column_of(vm_ref[part], vo_ref[part], j) for j in range(PACK)]
        values = jnp.concatenate(near_v + far_v, 0)
        left = jnp.concatenate([weights * picks[j] for j in range(PACK)], 0)
        context = dot(left, values)
        for j in range(PACK):
            outs = []
            for t in range(heads // 2):
                lanes = slice(t * 2 * HEAD_DIM, (t + 1) * 2 * HEAD_DIM)
                at = j * rows + t * pair
                head = t * pair
                out = jnp.where(
                    left_head,
                    context[at : at + BOTH, lanes],
                    context[at + BOTH : at + 2 * BOTH, lanes],
                )
                factor = jnp.where(
                    left_head,
                    inverse[head : head + BOTH, j : j + 1],
                    inverse[head + BOTH : head + 2 * BOTH, j : j + 1],
                )
                outs.append((out * factor).astype(BF16))
            out = jnp.concatenate(outs, 1)
            om_ref[g * PACK + j] = out[:STRIP]
            oo_ref[g * PACK + j] = out[STRIP:]

    by_pack(first, cols, body)


def column_part(info, mine, other, recv_mine, recv_other, weights, first, cols):
    width = mine.shape[-1]
    heads = width // HEAD_DIM
    shape = jax.ShapeDtypeStruct((cols, STRIP, width), BF16)
    return call(
        functools.partial(column_kernel, heads=heads, first=first, cols=cols),
        info,
        [mine, other, recv_mine, recv_other, weights],
        [shape, shape],
        [pltpu.VMEM((2, cols, heads * BOTH), F32)],
        name="column_attention",
    )


def mix_kernel(info, *refs, first, cols, parts):
    row_refs, near_ref, far_ref = refs[:parts], refs[parts], refs[parts + 1]
    out_ref, out_buf, out_sem = refs[-3:]
    copies = []
    for o, ref in enumerate((near_ref, far_ref)):
        span = column_span(info, o == 1, first, cols)
        column = jnp.swapaxes(ref[...], 0, 1).astype(F32)
        at = 0
        for row_ref in row_refs:
            rows = slice(at, at + row_ref.shape[0])
            out_buf[o, rows] = (0.5 * (row_ref[:, span, :] + column[rows])).astype(BF16)
            at += row_ref.shape[0]
        copy = pltpu.make_async_copy(out_buf.at[o], out_ref.at[:, span, :], out_sem.at[o])
        copy.start()
        copies.append(copy)
    for copy in copies:
        copy.wait()


def mix(info, row_context, near, far, done, first):
    cols, _, width = near.shape
    parts = len(row_context)
    operands = list(row_context) + [near, far]
    in_specs = [ON_CHIP] * len(operands)
    aliases = {}
    if done is not None:
        operands.append(done)
        in_specs.append(ANYWHERE)
        aliases = {len(operands): 0}
    return call(
        functools.partial(mix_kernel, first=first, cols=cols, parts=parts),
        info,
        operands,
        jax.ShapeDtypeStruct((STRIP, COLS, width), BF16),
        [pltpu.VMEM((2, STRIP, cols, width), BF16), pltpu.SemaphoreType.DMA((2,))],
        in_specs=in_specs,
        out_specs=ANYWHERE,
        aliases=aliases,
        name="mix",
    )


CORE_SWAP = [(0, 1), (1, 0), (2, 3), (3, 2)]
SAME_CORE = [(0, 2), (1, 3), (2, 0), (3, 1)]
OTHER_CORE = [(0, 3), (1, 2), (2, 1), (3, 0)]
DOWN_SAME = [(0, 2), (1, 3)]
UP_SAME = [(2, 0), (3, 1)]
NEXT_STRIP = [(0, 1), (1, 2), (2, 3)]


def send(block, route):
    return pltpu.with_memory_space_constraint(lax.ppermute(block, "seq", route), pltpu.VMEM)


def in_hbm(array):
    return pltpu.with_memory_space_constraint(array, pltpu.HBM)


def after(value, *earlier):
    return lax.optimization_barrier((value,) + earlier)[0]


def two_chips(patches, w_qkv):
    width = w_qkv.shape[2]
    chunks = ((0, 64), (64, 64))
    seq = lax.axis_index("seq")
    info = jnp.stack([seq % 2, seq // 2, seq]).astype(jnp.int32)
    x = patches.reshape(STRIP, COLS, D)
    w = jnp.transpose(w_qkv, (1, 0, 2))

    first = project(info, in_hbm(x), in_hbm(w))
    recv_mine = send(first[4], SAME_CORE)
    natural, mine, other, last = project_rest(info, first[6], w, first[:4])
    other = send(other, CORE_SWAP)
    halo = send(last, NEXT_STRIP)
    recv_other = send(after(first[5], last), OTHER_CORE)
    info = after(info, recv_mine, halo)
    rows_low = row_part(info, None, natural, 8, 8)
    info = after(info, rows_low)
    rows_top = row_part(info, halo, natural, 0, 8)
    info = after(info, rows_top)
    top = maxima(info, mine, other)
    below = send(top, UP_SAME)
    info = after(info, top)
    far = []
    for at, cols in chunks:
        weights = cross_weights(info, recv_mine, recv_other, mine, other, below, at, cols)
        info = after(info, weights)
        far.append(send(weights, DOWN_SAME))
    out = None
    for (at, cols), weights in zip(chunks, far):
        near, remote = column_part(info, mine, other, recv_mine, recv_other, weights, at, cols)
        remote = send(remote, CORE_SWAP)
        out = mix(info, (rows_top, rows_low), near, remote, out, at)
        info = after(info, out)
    return out.reshape(STRIP * COLS, width)


def local(patches, w_qkv):
    shape_fits = patches.shape[0] == STRIP * COLS and w_qkv.shape[2] == 4 * HEAD_DIM
    if lax.axis_size("seq") == 4 and shape_fits:
        return two_chips(patches, w_qkv)
    return general(patches, w_qkv)


def solution(mesh):
    placed = (P(("groups", "seq"), None), P(None, None, "head"))
    return jax.shard_map(
        local, mesh=mesh, in_specs=placed, out_specs=P(("groups", "seq"), "head"), check_vma=False
    )
```

profile of v0, /device:TPU:5, one launch (start us, length us, event | category | flops | bytes accessed | tf_op | source)
XLA Modules:
  0.0 99.2 jit_solution(13466288994008696402)
XLA Ops:
  0.0 0.1 pad_add_fusion.info
  0.1 0.0 copy-start
  0.1 7.3 %project_sent.1 = (bf16[3,16,256,256]{3,2,1,0:T(8,128)(2,1)S(1)}, bf16[3,128,16,256]{3,2,1,0:T(8,128)(2,1)S(1)}, bf16[3,128,16,256]{3,2,1,0:T(8,128)(2,1)S(1)}, ...) custom-call(s32[3]{0:T(128)S(1)} %pad_add_fusion.info, ...), custom_call_target="tpu_custom_call" | custom-call | flops 1 | bytes 1 | tf_op jit(solution)/shard_map/project_sent/pallas_call | solution.py:144
  7.4 0.1 collective-permute-start
  7.4 0.0 copy-done
  7.4 6.8 %project_rest.1 = (bf16[3,16,256,256]{3,2,1,0:T(8,128)(2,1)S(1)}, bf16[3,128,16,256]{3,2,1,0:T(8,128)(2,1)S(1)}, bf16[3,128,16,256]{3,2,1,0:T(8,128)(2,1)S(1)}, bf16[2,256,256]{2,1,0:T(8,128)(2,1)S(1)}) custom-call(s32[3]{0:T(128)S(1)} %pad_add_fusion.info, ...), custom_call_target="tpu_custom_call", output_to_operand_aliasing={{0}: (3, {}), {1}: (4, {}), {2}: (5, {}), {3}: (6, {})} | custom-call | flops 1 | bytes 1 | tf_op jit(solution)/shard_map/project_rest/pallas_call | solution.py:144
  14.2 1.5 %collective-permute-start.1 = (bf16[2,256,256]{2,1,0:T(8,128)(2,1)S(1)}, bf16[2,256,256]{2,1,0:T(8,128)(2,1)S(1)}, u32[]{:S(2)}, u32[]{:S(2)}) collective-permute-start(bf16[2,256,256]{2,1,0:T(8,128)(2,1)S(1)} %get-tuple-element.34), channel_id=1, source_target_pairs={{0,4},{4,8},{8,12},{1,5},{5,9},{9,13},{2,6},{6,10},{10,14},{3,7},{... | collective-permute-start | bytes 786440 | tf_op jit(solution)/shard_map/ppermute | solution.py:573
  15.7 2.5 %collective-permute-start.3 = (bf16[128,16,256]{2,1,0:T(8,128)(2,1)S(1)}, bf16[128,16,256]{2,1,0:T(8,128)(2,1)S(1)}, u32[]{:S(2)}, u32[]{:S(2)}) collective-permute-start(bf16[128,16,256]{2,1,0:T(8,128)(2,1)S(1)} %get-tuple-element.43), channel_id=1, source_target_pairs={{0,12},{4,8},{8,4},{12,0},{1,13},{5,9},{9,5},{13,1},{2,14},{6,10},... | collective-permute-start | bytes 3145736 | tf_op jit(solution)/shard_map/ppermute | solution.py:573
  18.2 0.6 collective-permute-start.2
  18.8 0.0 collective-permute-done.1.refs_0_.refs_1_
  18.8 12.7 %collective-permute-done.qm_ref.vm_ref = bf16[128,16,256]{2,1,0:T(8,128)(2,1)S(1)} collective-permute-done((bf16[128,16,256]{2,1,0:T(8,128)(2,1)S(1)}, bf16[128,16,256]{2,1,0:T(8,128)(2,1)S(1)}, u32[]{:S(2)}, u32[]{:S(2)}) %collective-permute-start) | collective-permute-done | bytes 1048608 | tf_op jit(solution)/shard_map/ppermute | solution.py:573
  31.4 6.3 %row_attention.2.refs_1_ = f32[8,256,256]{2,1,0:T(8,128)S(1)} custom-call(s32[3]{0:T(128)S(1)} %pad_add_fusion.info, bf16[3,16,256,256]{3,2,1,0:T(8,128)(2,1)S(1)} %get-tuple-element.36.refs_0_.refs_1_.refs_2_.refs_3_.refs_4_, bf16[3,16,256,256]{3,2,1,0:T(8,128)(2,1)S(1)} %get-tuple-element.36.refs_0_.refs_1_.refs_2_.refs_3_.refs_4_, ...), custom_call_target="tpu_custom_call" | custom-call | flops 20000000000 | bytes 1 | tf_op jit(solution)/shard_map/row_attention/pallas_call | solution.py:144
  37.7 6.3 %row_attention.3.refs_0_ = f32[8,256,256]{2,1,0:T(8,128)S(1)} custom-call(s32[3]{0:T(128)S(1)} %pad_add_fusion.info, bf16[2,256,256]{2,1,0:T(8,128)(2,1)S(1)} %collective-permute-done.1.refs_0_.refs_1_, bf16[2,256,256]{2,1,0:T(8,128)(2,1)S(1)} %collective-permute-done.1.refs_0_.refs_1_, ...), custom_call_target="tpu_custom_call" | custom-call | flops 20000000000 | bytes 1 | tf_op jit(solution)/shard_map/row_attention/pallas_call | solution.py:144
  44.1 0.0 collective-permute-done.2.other_ref
  44.1 4.3 %maxima.1 = f32[128,128]{1,0:T(8,128)S(1)} custom-call(s32[3]{0:T(128)S(1)} %pad_add_fusion.info, bf16[3,128,16,256]{3,2,1,0:T(8,128)(2,1)S(1)} %get-tuple-element.39.mine_ref, bf16[3,128,16,256]{3,2,1,0:T(8,128)(2,1)S(1)} %collective-permute-done.2.other_ref), custom_call_target="tpu_custom_call" | custom-call | flops 1 | bytes 1 | tf_op jit(solution)/shard_map/maxima/pallas_call | solution.py:144
  48.4 3.1 %collective-permute-start.4 = (f32[128,128]{1,0:T(8,128)S(1)}, f32[128,128]{1,0:T(8,128)S(1)}, u32[]{:S(2)}, u32[]{:S(2)}) collective-permute-start(f32[128,128]{1,0:T(8,128)S(1)} %maxima.1), channel_id=1, source_target_pairs={{8,0},{12,4},{9,1},{13,5},{10,2},{14,6},{11,3},{15,7},{24,16},{28,... | collective-permute-start | bytes 196616 | tf_op jit(solution)/shard_map/ppermute | solution.py:573
  51.5 4.8 %collective-permute-done.3.qo_ref.vo_ref = bf16[128,16,256]{2,1,0:T(8,128)(2,1)S(1)} collective-permute-done((bf16[128,16,256]{2,1,0:T(8,128)(2,1)S(1)}, bf16[128,16,256]{2,1,0:T(8,128)(2,1)S(1)}, u32[]{:S(2)}, u32[]{:S(2)}) %collective-permute-start.3) | collective-permute-done | bytes 1048608 | tf_op jit(solution)/shard_map/ppermute | solution.py:573
  56.2 0.0 collective-permute-done.4.top_ref
  56.2 0.6 cross_weights.2
  56.8 1.3 %collective-permute-start.5 = (bf16[2432,128]{1,0:T(8,128)(2,1)S(1)}, bf16[2432,128]{1,0:T(8,128)(2,1)S(1)}, u32[]{:S(2)}, u32[]{:S(2)}) collective-permute-start(bf16[2432,128]{1,0:T(8,128)(2,1)S(1)} %cross_weights.2), channel_id=1, source_target_pairs={{0,8},{4,12},{1,9},{5,13},{2,10},{6,14},{3,11},{7,15},{16,24},{20,... | collective-permute-start | bytes 1867784 | tf_op jit(solution)/shard_map/ppermute | solution.py:573
  58.1 0.6 cross_weights.3
  58.7 1.3 %collective-permute-start.7 = (bf16[2432,128]{1,0:T(8,128)(2,1)S(1)}, bf16[2432,128]{1,0:T(8,128)(2,1)S(1)}, u32[]{:S(2)}, u32[]{:S(2)}) collective-permute-start(bf16[2432,128]{1,0:T(8,128)(2,1)S(1)} %cross_weights.3), channel_id=1, source_target_pairs={{0,8},{4,12},{1,9},{5,13},{2,10},{6,14},{3,11},{7,15},{16,24},{20,... | collective-permute-start | bytes 1867784 | tf_op jit(solution)/shard_map/ppermute | solution.py:573
  60.0 13.1 %collective-permute-done.5.w_ref = bf16[2432,128]{1,0:T(8,128)(2,1)S(1)} collective-permute-done((bf16[2432,128]{1,0:T(8,128)(2,1)S(1)}, bf16[2432,128]{1,0:T(8,128)(2,1)S(1)}, u32[]{:S(2)}, u32[]{:S(2)}) %collective-permute-start.5) | collective-permute-done | bytes 622624 | tf_op jit(solution)/shard_map/ppermute | solution.py:573
  73.1 6.0 %column_attention.2 = (bf16[64,16,256]{2,1,0:T(8,128)(2,1)S(1)}, bf16[64,16,256]{2,1,0:T(8,128)(2,1)S(1)}) custom-call(s32[3]{0:T(128)S(1)} %pad_add_fusion.info, bf16[3,128,16,256]{3,2,1,0:T(8,128)(2,1)S(1)} %get-tuple-element.39.mine_ref, bf16[3,128,16,256]{3,2,1,0:T(8,128)(2,1)S(1)} %collective-permute-done.2.other_ref, ...), custom_call_target="tpu_custom_call" | custom-call | flops 1 | bytes 1 | tf_op jit(solution)/shard_map/column_attention/pallas_call | solution.py:144
  79.1 6.0 %collective-permute-start.6 = (bf16[64,16,256]{2,1,0:T(8,128)(2,1)S(1)}, bf16[64,16,256]{2,1,0:T(8,128)(2,1)S(1)}, u32[]{:S(2)}, u32[]{:S(2)}) collective-permute-start(bf16[64,16,256]{2,1,0:T(8,128)(2,1)S(1)} %get-tuple-element.47), channel_id=1, source_target_pairs={{0,4},{4,0},{8,12},{12,8},{1,5},{5,1},{9,13},{13,9},{2,6},{6,2},{1... | collective-permute-start | bytes 1572872 | tf_op jit(solution)/shard_map/ppermute | solution.py:573
  85.0 1.5 %collective-permute-done.6.refs_3_ = bf16[64,16,256]{2,1,0:T(8,128)(2,1)S(1)} collective-permute-done((bf16[64,16,256]{2,1,0:T(8,128)(2,1)S(1)}, bf16[64,16,256]{2,1,0:T(8,128)(2,1)S(1)}, u32[]{:S(2)}, u32[]{:S(2)}) %collective-permute-start.6) | collective-permute-done | bytes 524320 | tf_op jit(solution)/shard_map/ppermute | solution.py:573
  86.6 1.9 %mix.2.refs_4_ = bf16[16,256,256]{2,1,0:T(8,128)(2,1)} custom-call(s32[3]{0:T(128)S(1)} %pad_add_fusion.info, f32[8,256,256]{2,1,0:T(8,128)S(1)} %row_attention.3.refs_0_, f32[8,256,256]{2,1,0:T(8,128)S(1)} %row_attention.2.refs_1_, bf16[64,16,256]{2,1,0:T(8,128)(2,1)S(1)} %get-tuple-element.46.refs_2_, bf16[64,16,256]{2,1,0:T(8,128)(2,1)S(1)} %collective-permute-done.6.refs_3_), custom_call_target="tpu_custom_call" | custom-call | flops 1 | bytes 1 | tf_op jit(solution)/shard_map/mix/pallas_call | solution.py:144
  88.4 0.0 collective-permute-done.7.w_ref
  88.4 6.0 %column_attention.3 = (bf16[64,16,256]{2,1,0:T(8,128)(2,1)S(1)}, bf16[64,16,256]{2,1,0:T(8,128)(2,1)S(1)}) custom-call(s32[3]{0:T(128)S(1)} %pad_add_fusion.info, bf16[3,128,16,256]{3,2,1,0:T(8,128)(2,1)S(1)} %get-tuple-element.39.mine_ref, bf16[3,128,16,256]{3,2,1,0:T(8,128)(2,1)S(1)} %collective-permute-done.2.other_ref, ...), custom_call_target="tpu_custom_call" | custom-call | flops 1 | bytes 1 | tf_op jit(solution)/shard_map/column_attention/pallas_call | solution.py:144
  94.4 1.2 %collective-permute-start.8 = (bf16[64,16,256]{2,1,0:T(8,128)(2,1)S(1)}, bf16[64,16,256]{2,1,0:T(8,128)(2,1)S(1)}, u32[]{:S(2)}, u32[]{:S(2)}) collective-permute-start(bf16[64,16,256]{2,1,0:T(8,128)(2,1)S(1)} %get-tuple-element.50), channel_id=1, source_target_pairs={{0,4},{4,0},{8,12},{12,8},{1,5},{5,1},{9,13},{13,9},{2,6},{6,2},{1... | collective-permute-start | bytes 1572872 | tf_op jit(solution)/shard_map/ppermute | solution.py:573
  95.6 1.5 %collective-permute-done.8.refs_3_ = bf16[64,16,256]{2,1,0:T(8,128)(2,1)S(1)} collective-permute-done((bf16[64,16,256]{2,1,0:T(8,128)(2,1)S(1)}, bf16[64,16,256]{2,1,0:T(8,128)(2,1)S(1)}, u32[]{:S(2)}, u32[]{:S(2)}) %collective-permute-start.8) | collective-permute-done | bytes 524320 | tf_op jit(solution)/shard_map/ppermute | solution.py:573
  97.2 1.9 %mix.3 = bf16[16,256,256]{2,1,0:T(8,128)(2,1)} custom-call(s32[3]{0:T(128)S(1)} %pad_add_fusion.info, f32[8,256,256]{2,1,0:T(8,128)S(1)} %row_attention.3.refs_0_, f32[8,256,256]{2,1,0:T(8,128)S(1)} %row_attention.2.refs_1_, bf16[64,16,256]{2,1,0:T(8,128)(2,1)S(1)} %get-tuple-element.49.refs_2_, ...), custom_call_target="tpu_custom_call", output_to_operand_aliasing={{}: (5, {})} | custom-call | flops 1 | bytes 1 | tf_op jit(solution)/shard_map/mix/pallas_call | solution.py:144
Async XLA Ops:
  0.1 7.4 %copy-start = (bf16[1024,3,256]{2,0,1:T(8,128)(2,1)S(1)}, bf16[1024,3,256]{2,0,1:T(8,128)(2,1)}, u32[]{:S(2)}) copy-start(bf16[1024,3,256]{2,0,1:T(8,128)(2,1)} %param.3) | copy-start | bytes 4718596
  7.4 24.1 %collective-permute-start = (bf16[128,16,256]{2,1,0:T(8,128)(2,1)S(1)}, bf16[128,16,256]{2,1,0:T(8,128)(2,1)S(1)}, u32[]{:S(2)}, u32[]{:S(2)}) collective-permute-start(bf16[128,16,256]{2,1,0:T(8,128)(2,1)S(1)} %get-tuple-element.28), channel_id=1, source_target_pairs={{0,8},{4,12},{8,0},{12,4},{1,9},{5,13},{9,1},{13,5},{2,10},{6,14},... | collective-permute-start | bytes 3145736 | tf_op jit(solution)/shard_map/ppermute | solution.py:573
  14.2 4.6 %collective-permute-start.1 = (bf16[2,256,256]{2,1,0:T(8,128)(2,1)S(1)}, bf16[2,256,256]{2,1,0:T(8,128)(2,1)S(1)}, u32[]{:S(2)}, u32[]{:S(2)}) collective-permute-start(bf16[2,256,256]{2,1,0:T(8,128)(2,1)S(1)} %get-tuple-element.34), channel_id=1, source_target_pairs={{0,4},{4,8},{8,12},{1,5},{5,9},{9,13},{2,6},{6,10},{10,14},{3,7},{... | collective-permute-start | bytes 786440 | tf_op jit(solution)/shard_map/ppermute | solution.py:573
  15.7 40.5 %collective-permute-start.3 = (bf16[128,16,256]{2,1,0:T(8,128)(2,1)S(1)}, bf16[128,16,256]{2,1,0:T(8,128)(2,1)S(1)}, u32[]{:S(2)}, u32[]{:S(2)}) collective-permute-start(bf16[128,16,256]{2,1,0:T(8,128)(2,1)S(1)} %get-tuple-element.43), channel_id=1, source_target_pairs={{0,12},{4,8},{8,4},{12,0},{1,13},{5,9},{9,5},{13,1},{2,14},{6,10},... | collective-permute-start | bytes 3145736 | tf_op jit(solution)/shard_map/ppermute | solution.py:573
  18.2 25.8 %collective-permute-start.2 = (bf16[3,128,16,256]{3,2,1,0:T(8,128)(2,1)S(1)}, bf16[3,128,16,256]{3,2,1,0:T(8,128)(2,1)S(1)}, u32[]{:S(2)}, u32[]{:S(2)}) collective-permute-start(bf16[3,128,16,256]{3,2,1,0:T(8,128)(2,1)S(1)} %get-tuple-element.40), channel_id=1, source_target_pairs={{0,4},{4,0},{8,12},{12,8},{1,5},{5,1},{9,13},{13,9},{2,6},{6,2},{1... | collective-permute-start | bytes 9437192 | tf_op jit(solution)/shard_map/ppermute | solution.py:573
  48.4 7.8 %collective-permute-start.4 = (f32[128,128]{1,0:T(8,128)S(1)}, f32[128,128]{1,0:T(8,128)S(1)}, u32[]{:S(2)}, u32[]{:S(2)}) collective-permute-start(f32[128,128]{1,0:T(8,128)S(1)} %maxima.1), channel_id=1, source_target_pairs={{8,0},{12,4},{9,1},{13,5},{10,2},{14,6},{11,3},{15,7},{24,16},{28,... | collective-permute-start | bytes 196616 | tf_op jit(solution)/shard_map/ppermute | solution.py:573
  56.8 16.3 %collective-permute-start.5 = (bf16[2432,128]{1,0:T(8,128)(2,1)S(1)}, bf16[2432,128]{1,0:T(8,128)(2,1)S(1)}, u32[]{:S(2)}, u32[]{:S(2)}) collective-permute-start(bf16[2432,128]{1,0:T(8,128)(2,1)S(1)} %cross_weights.2), channel_id=1, source_target_pairs={{0,8},{4,12},{1,9},{5,13},{2,10},{6,14},{3,11},{7,15},{16,24},{20,... | collective-permute-start | bytes 1867784 | tf_op jit(solution)/shard_map/ppermute | solution.py:573
  58.7 29.8 %collective-permute-start.7 = (bf16[2432,128]{1,0:T(8,128)(2,1)S(1)}, bf16[2432,128]{1,0:T(8,128)(2,1)S(1)}, u32[]{:S(2)}, u32[]{:S(2)}) collective-permute-start(bf16[2432,128]{1,0:T(8,128)(2,1)S(1)} %cross_weights.3), channel_id=1, source_target_pairs={{0,8},{4,12},{1,9},{5,13},{2,10},{6,14},{3,11},{7,15},{16,24},{20,... | collective-permute-start | bytes 1867784 | tf_op jit(solution)/shard_map/ppermute | solution.py:573
  79.1 7.5 %collective-permute-start.6 = (bf16[64,16,256]{2,1,0:T(8,128)(2,1)S(1)}, bf16[64,16,256]{2,1,0:T(8,128)(2,1)S(1)}, u32[]{:S(2)}, u32[]{:S(2)}) collective-permute-start(bf16[64,16,256]{2,1,0:T(8,128)(2,1)S(1)} %get-tuple-element.47), channel_id=1, source_target_pairs={{0,4},{4,0},{8,12},{12,8},{1,5},{5,1},{9,13},{13,9},{2,6},{6,2},{1... | collective-permute-start | bytes 1572872 | tf_op jit(solution)/shard_map/ppermute | solution.py:573
  94.4 2.7 %collective-permute-start.8 = (bf16[64,16,256]{2,1,0:T(8,128)(2,1)S(1)}, bf16[64,16,256]{2,1,0:T(8,128)(2,1)S(1)}, u32[]{:S(2)}, u32[]{:S(2)}) collective-permute-start(bf16[64,16,256]{2,1,0:T(8,128)(2,1)S(1)} %get-tuple-element.50), channel_id=1, source_target_pairs={{0,4},{4,0},{8,12},{12,8},{1,5},{5,1},{9,13},{13,9},{2,6},{6,2},{1... | collective-permute-start | bytes 1572872 | tf_op jit(solution)/shard_map/ppermute | solution.py:573
where the time goes:
time: 99.6 us; the launch traced here: 99.2 us
  Pallas kernels  47.7 us (48%)
  waiting for transfers between devices  33.6 us (34%)
  starting transfers between devices  17.5 us (18%)
    pallas_call x11, Pallas kernels, call(): pl.pallas_call(kernel, out_shape=out_shape, grid_spec=pltpu.PrefetchScala...  47.7 us
    ppermute x9, waiting for transfers between devices, send(): lax.ppermute(block, 'seq', route)  33.6 us
    ppermute x9, starting transfers between devices, send(): lax.ppermute(block, 'seq', route)  17.5 us
  transfers between devices with their start and end apart: 9, of which 5 were waited for; matrix products, arithmetic and copies ran while one was open for 0% of the time, Pallas kernels for 32%

commit v1 on v0

--- a/solution.py
+++ b/solution.py
@@ -128,6 +128,8 @@
 
 SLICES = 3
 HALF = COLS // 2
+LONG = 4 * 10**10
+SPLIT = HALF // 2
 ANYWHERE = pl.BlockSpec(memory_space=pl.ANY)
 ON_CHIP = pl.BlockSpec(memory_space=pltpu.VMEM)
 
@@ -166,7 +168,7 @@
     return jnp.where(info[1] == 0, 2, 0)
 
 
-def projected(x, w, natural_ref, last_ref, turned_refs, slot, columns, rows):
+def projected(x, w, natural_ref, last_ref, turned_refs, slot, columns):
     _, block, depth = x.shape
     part = STRIP // 2
     parts = [
@@ -181,12 +183,12 @@
 
     turned = jnp.swapaxes(value, 0, 1)
     for ref in turned_refs:
-        ref[rows] = turned
+        ref[...] = turned
 
 
 def first_kernel(info, x_ref, w_ref, *refs, block):
-    natural_ref, mine_ref, other_ref, last_ref, send_mine_ref, send_other_ref, x_out = refs[:7]
-    w_buf, x_sem, w_sem = refs[7:]
+    natural_ref, mine_ref, other_ref, last_ref, send_mine_ref = refs[:5]
+    send_others, x_out, w_buf, x_sem, w_sem = refs[5:7], refs[7], *refs[8:]
     slot = sent_slot(info)
     w_copy = pltpu.make_async_copy(w_ref.at[slot], w_buf, w_sem)
     w_copy.start()
@@ -204,16 +206,18 @@
     for copy, other, first, columns in pieces:
         copy.wait()
         triple_ref = other_ref if other else mine_ref
-        send_ref = send_other_ref if other else send_mine_ref
+        if other:
+            send_ref = send_others[first // SPLIT].at[pl.ds(first % SPLIT, block)]
+        else:
+            send_ref = send_mine_ref.at[pl.ds(first, block)]
         projected(
             x_out[:, columns, :],
             w,
             natural_ref,
             last_ref,
-            (triple_ref.at[slot], send_ref),
+            (triple_ref.at[slot, pl.ds(first, block)], send_ref),
             slot,
             columns,
-            pl.ds(first, block),
         )
 
 
@@ -229,10 +233,9 @@
                     w,
                     natural_ref,
                     last_ref,
-                    (triple_ref.at[slot],),
+                    (triple_ref.at[slot, pl.ds(first, block)],),
                     slot,
                     columns,
-                    pl.ds(first, block),
                 )
 
 
@@ -241,12 +244,12 @@
     natural = jax.ShapeDtypeStruct((3, STRIP, COLS, width), BF16)
     triple = jax.ShapeDtypeStruct((3, HALF, STRIP, width), BF16)
     last = jax.ShapeDtypeStruct((2, COLS, width), BF16)
-    single = jax.ShapeDtypeStruct((HALF, STRIP, width), BF16)
+    sends = [jax.ShapeDtypeStruct((n, STRIP, width), BF16) for n in (HALF, SPLIT, HALF - SPLIT)]
     return call(
         functools.partial(first_kernel, block=block),
         info,
         [x, w],
-        [natural, triple, triple, last, single, single, jax.ShapeDtypeStruct(x.shape, BF16)],
+        [natural, triple, triple, last] + sends + [jax.ShapeDtypeStruct(x.shape, BF16)],
         [
             pltpu.VMEM(w.shape[1:], BF16),
             pltpu.SemaphoreType.DMA((COLS // block,)),
@@ -337,7 +340,7 @@
         grid=(row_count // rows,),
         in_specs=[before_spec(1), before_spec(2)] + [spec(slot) for slot in range(3)],
         out_specs=pl.BlockSpec((rows, COLS, width), lambda r, info: (r, 0, 0)),
-        flops=2 * 10**10,
+        flops=LONG,
         name="row_attention",
     )
 
@@ -395,12 +398,12 @@
 
 
 def weights_kernel(
-    info, qm_ref, qo_ref, mine_ref, other_ref, top_ref, w_ref, stats, *, heads, first, cols
+    info, qm_ref, qo_ref, mine_ref, other_ref, top_ref, w_ref, stats, *, heads, first, cols, base
 ):
     spread = head_rows(BOTH, heads * HEAD_DIM)
 
     def body(g, part):
-        qm, qo = qm_ref[part], qo_ref[part]
+        qm, qo = qm_ref[part], qo_ref[pl.ds(first - base + g * PACK, PACK)]
         km, ko = mine_ref[1, part], other_ref[1, part]
         below = top_ref[part]
         tops, totals, turned = [], [], []
@@ -426,11 +429,11 @@
             rest = rest - part.astype(F32)
 
 
-def cross_weights(info, recv_mine, recv_other, mine, other, top, first, cols):
+def cross_weights(info, recv_mine, recv_other, mine, other, top, first, cols, base):
     heads = mine.shape[-1] // HEAD_DIM
     rows = heads * BOTH
     return call(
-        functools.partial(weights_kernel, heads=heads, first=first, cols=cols),
+        functools.partial(weights_kernel, heads=heads, first=first, cols=cols, base=base),
         info,
         [recv_mine, recv_other, mine, other, top],
         jax.ShapeDtypeStruct((cols // PACK * rows + SLICES * 2 * cols, PACK * BOTH), BF16),
@@ -440,7 +443,7 @@
 
 
 def column_kernel(
-    info, mine_ref, other_ref, vm_ref, vo_ref, w_ref, om_ref, oo_ref, stats, *, heads, first, cols
+    info, mine_ref, other_ref, vm_ref, vo_ref, w_ref, om_ref, oo_ref, stats, *, heads, first, cols, base
 ):
     hidden = later_key(info[0], heads)
     width = heads * HEAD_DIM
@@ -477,7 +480,8 @@
         near = jnp.concatenate(turned, 0).T.astype(BF16)
         weights = jnp.concatenate([near, w_ref[pl.ds(g * rows, rows)]], 1)
         near_v = [column_of(mine_ref[2, part], other_ref[2, part], j) for j in range(PACK)]
-        far_v = [column_of(vm_ref[part], vo_ref[part], j) for j in range(PACK)]
+        vm, vo = vm_ref[part], vo_ref[pl.ds(first - base + g * PACK, PACK)]
+        far_v = [column_of(vm, vo, j) for j in range(PACK)]
         values = jnp.concatenate(near_v + far_v, 0)
         left = jnp.concatenate([weights * picks[j] for j in range(PACK)], 0)
         context = dot(left, values)
@@ -505,16 +509,17 @@
     by_pack(first, cols, body)
 
 
-def column_part(info, mine, other, recv_mine, recv_other, weights, first, cols):
+def column_part(info, mine, other, recv_mine, recv_other, weights, first, cols, base, flops):
     width = mine.shape[-1]
     heads = width // HEAD_DIM
     shape = jax.ShapeDtypeStruct((cols, STRIP, width), BF16)
     return call(
-        functools.partial(column_kernel, heads=heads, first=first, cols=cols),
+        functools.partial(column_kernel, heads=heads, first=first, cols=cols, base=base),
         info,
         [mine, other, recv_mine, recv_other, weights],
         [shape, shape],
         [pltpu.VMEM((2, cols, heads * BOTH), F32)],
+        flops=flops,
         name="column_attention",
     )
 
@@ -583,7 +588,7 @@
 
 def two_chips(patches, w_qkv):
     width = w_qkv.shape[2]
-    chunks = ((0, 64), (64, 64))
+    chunks = ((0, 64), (64, 32), (96, 32))
     seq = lax.axis_index("seq")
     info = jnp.stack([seq % 2, seq // 2, seq]).astype(jnp.int32)
     x = patches.reshape(STRIP, COLS, D)
@@ -591,29 +596,53 @@
 
     first = project(info, in_hbm(x), in_hbm(w))
     recv_mine = send(first[4], SAME_CORE)
-    natural, mine, other, last = project_rest(info, first[6], w, first[:4])
+    natural, mine, other, last = project_rest(info, first[7], w, first[:4])
     other = send(other, CORE_SWAP)
     halo = send(last, NEXT_STRIP)
-    recv_other = send(after(first[5], last), OTHER_CORE)
+    recv_others = [send(after(first[5], last), OTHER_CORE)]
     info = after(info, recv_mine, halo)
     rows_low = row_part(info, None, natural, 8, 8)
     info = after(info, rows_low)
-    rows_top = row_part(info, halo, natural, 0, 8)
-    info = after(info, rows_top)
     top = maxima(info, mine, other)
     below = send(top, UP_SAME)
+    recv_others.append(send(after(first[6], top), OTHER_CORE))
     info = after(info, top)
     far = []
-    for at, cols in chunks:
-        weights = cross_weights(info, recv_mine, recv_other, mine, other, below, at, cols)
+    for n, (at, cols) in enumerate(chunks):
+        part = at // SPLIT
+        weights = cross_weights(
+            info, recv_mine, recv_others[part], mine, other, below, at, cols, part * SPLIT
+        )
         info = after(info, weights)
         far.append(send(weights, DOWN_SAME))
+        if n == 0:
+            rows_top = row_part(info, halo, natural, 0, 8)
+            info = after(info, rows_top)
+    row_context = (rows_top, rows_low)
+    pending = []
     out = None
-    for (at, cols), weights in zip(chunks, far):
-        near, remote = column_part(info, mine, other, recv_mine, recv_other, weights, at, cols)
-        remote = send(remote, CORE_SWAP)
-        out = mix(info, (rows_top, rows_low), near, remote, out, at)
-        info = after(info, out)
+    for n, ((at, cols), weights) in enumerate(zip(chunks, far)):
+        part = at // SPLIT
+        near, remote = column_part(
+            info,
+            mine,
+            other,
+            recv_mine,
+            recv_others[part],
+            weights,
+            at,
+            cols,
+            part * SPLIT,
+            LONG if n > 0 else 1,
+        )
+        info = after(info, near)
+        pending.append((near, send(remote, CORE_SWAP), at))
+        if n > 0:
+            near, remote, at = pending.pop(0)
+            out = mix(info, row_context, near, remote, out, at)
+            info = after(info, out)
+    near, remote, at = pending.pop(0)
+    out = mix(info, row_context, near, remote, out, at)
     return out.reshape(STRIP * COLS, width)
 
 

time: 99.6 us -> 93.6 us (0.940)
  starting transfers between devices: 17.5 us -> 13 us
  waiting for transfers between devices: 33.6 us -> 29.9 us
  Pallas kernels: 47.7 us -> 50 us
    ppermute x9 -> x12, starting transfers between devices: 17.5 us -> 13 us  [send(): lax.ppermute(block, 'seq', route)]
    ppermute x9 -> x12, waiting for transfers between devices: 33.6 us -> 29.9 us  [send(): lax.ppermute(block, 'seq', route)]
    pallas_call x11 -> x14, Pallas kernels: 47.7 us -> 50 us  [call(): pl.pallas_call(kernel, out_shape=out_shape, grid_spec=pltpu.PrefetchScala...]
  transfers between devices with their start and end apart: 9 -> 12, of which waited for: 5 -> 6; matrix products, arithmetic and copies ran while one was open for 0% -> 0% of each run, Pallas kernels for 32% -> 44%
where the time goes in v1:
time: 93.6 us; the launch traced here: 93.3 us
  Pallas kernels  50 us (53%)
  waiting for transfers between devices  29.9 us (32%)
  starting transfers between devices  13 us (14%)
    pallas_call x14, Pallas kernels, call(): pl.pallas_call(kernel, out_shape=out_shape, grid_spec=pltpu.PrefetchScala...  50 us
    ppermute x12, waiting for transfers between devices, send(): lax.ppermute(block, 'seq', route)  29.9 us
    ppermute x12, starting transfers between devices, send(): lax.ppermute(block, 'seq', route)  13 us
  transfers between devices with their start and end apart: 12, of which 6 were waited for; matrix products, arithmetic and copies ran while one was open for 0% of the time, Pallas kernels for 44%

profile of v1, /device:TPU:5, one launch (start us, length us, event | category | flops | bytes accessed | tf_op | source)
XLA Modules:
  0.0 93.3 jit_solution(16063000209404487721)
XLA Ops:
  0.0 0.1 pad_add_fusion.info
  0.1 7.3 %project_sent.1 = (bf16[3,16,256,256]{3,2,1,0:T(8,128)(2,1)S(1)}, bf16[3,128,16,256]{3,2,1,0:T(8,128)(2,1)S(1)}, bf16[3,128,16,256]{3,2,1,0:T(8,128)(2,1)S(1)}, ...) custom-call(s32[3]{0:T(128)S(1)} %pad_add_fusion.info, ...), custom_call_target="tpu_custom_call" | custom-call | flops 1 | bytes 1 | tf_op jit(solution)/shard_map/project_sent/pallas_call | solution.py:146
  7.4 0.1 collective-permute-start
  7.4 6.8 %project_rest.1 = (bf16[3,16,256,256]{3,2,1,0:T(8,128)(2,1)S(1)}, bf16[3,128,16,256]{3,2,1,0:T(8,128)(2,1)S(1)}, bf16[3,128,16,256]{3,2,1,0:T(8,128)(2,1)S(1)}, bf16[2,256,256]{2,1,0:T(8,128)(2,1)S(1)}) custom-call(s32[3]{0:T(128)S(1)} %pad_add_fusion.info, ...), custom_call_target="tpu_custom_call", output_to_operand_aliasing={{0}: (3, {}), {1}: (4, {}), {2}: (5, {}), {3}: (6, {})} | custom-call | flops 1 | bytes 1 | tf_op jit(solution)/shard_map/project_rest/pallas_call | solution.py:146
  14.2 1.3 %collective-permute-start.1 = (bf16[2,256,256]{2,1,0:T(8,128)(2,1)S(1)}, bf16[2,256,256]{2,1,0:T(8,128)(2,1)S(1)}, u32[]{:S(2)}, u32[]{:S(2)}) collective-permute-start(bf16[2,256,256]{2,1,0:T(8,128)(2,1)S(1)} %get-tuple-element.43), channel_id=1, source_target_pairs={{0,4},{4,8},{8,12},{1,5},{5,9},{9,13},{2,6},{6,10},{10,14},{3,7},{... | collective-permute-start | bytes 786440 | tf_op jit(solution)/shard_map/ppermute | solution.py:578
  15.5 2.5 %collective-permute-start.3 = (bf16[64,16,256]{2,1,0:T(8,128)(2,1)S(1)}, bf16[64,16,256]{2,1,0:T(8,128)(2,1)S(1)}, u32[]{:S(2)}, u32[]{:S(2)}) collective-permute-start(bf16[64,16,256]{2,1,0:T(8,128)(2,1)S(1)} %get-tuple-element.51), channel_id=1, source_target_pairs={{0,12},{4,8},{8,4},{12,0},{1,13},{5,9},{9,5},{13,1},{2,14},{6,10},... | collective-permute-start | bytes 1572872 | tf_op jit(solution)/shard_map/ppermute | solution.py:578
  18.1 0.6 collective-permute-start.2
  18.6 12.8 %collective-permute-done.qm_ref.vm_ref = bf16[128,16,256]{2,1,0:T(8,128)(2,1)S(1)} collective-permute-done((bf16[128,16,256]{2,1,0:T(8,128)(2,1)S(1)}, bf16[128,16,256]{2,1,0:T(8,128)(2,1)S(1)}, u32[]{:S(2)}, u32[]{:S(2)}) %collective-permute-start) | collective-permute-done | bytes 1048608 | tf_op jit(solution)/shard_map/ppermute | solution.py:578
  31.4 6.3 %row_attention.2.refs_1_ = f32[8,256,256]{2,1,0:T(8,128)S(1)} custom-call(s32[3]{0:T(128)S(1)} %pad_add_fusion.info, bf16[3,16,256,256]{3,2,1,0:T(8,128)(2,1)S(1)} %get-tuple-element.45.refs_0_.refs_1_.refs_2_.refs_3_.refs_4_, bf16[3,16,256,256]{3,2,1,0:T(8,128)(2,1)S(1)} %get-tuple-element.45.refs_0_.refs_1_.refs_2_.refs_3_.refs_4_, ...), custom_call_target="tpu_custom_call" | custom-call | flops 40000000000 | bytes 1 | tf_op jit(solution)/shard_map/row_attention/pallas_call | solution.py:146
  37.8 4.3 %maxima.1 = f32[128,128]{1,0:T(8,128)S(1)} custom-call(s32[3]{0:T(128)S(1)} %pad_add_fusion.info, bf16[3,128,16,256]{3,2,1,0:T(8,128)(2,1)S(1)} %get-tuple-element.47.mine_ref, bf16[3,128,16,256]{3,2,1,0:T(8,128)(2,1)S(1)} %collective-permute-done.2.other_ref), custom_call_target="tpu_custom_call" | custom-call | flops 1 | bytes 1 | tf_op jit(solution)/shard_map/maxima/pallas_call | solution.py:146
  42.1 3.1 %collective-permute-start.4 = (f32[128,128]{1,0:T(8,128)S(1)}, f32[128,128]{1,0:T(8,128)S(1)}, u32[]{:S(2)}, u32[]{:S(2)}) collective-permute-start(f32[128,128]{1,0:T(8,128)S(1)} %maxima.1), channel_id=1, source_target_pairs={{8,0},{12,4},{9,1},{13,5},{10,2},{14,6},{11,3},{15,7},{24,16},{28,... | collective-permute-start | bytes 196616 | tf_op jit(solution)/shard_map/ppermute | solution.py:578
  45.2 1.2 %collective-permute-done.4.top_ref = f32[128,128]{1,0:T(8,128)S(1)} collective-permute-done((f32[128,128]{1,0:T(8,128)S(1)}, f32[128,128]{1,0:T(8,128)S(1)}, u32[]{:S(2)}, u32[]{:S(2)}) %collective-permute-start.4) | collective-permute-done | bytes 65568 | tf_op jit(solution)/shard_map/ppermute | solution.py:578
  46.4 0.6 cross_weights.3
  47.0 1.5 %collective-permute-start.6 = (bf16[2432,128]{1,0:T(8,128)(2,1)S(1)}, bf16[2432,128]{1,0:T(8,128)(2,1)S(1)}, u32[]{:S(2)}, u32[]{:S(2)}) collective-permute-start(bf16[2432,128]{1,0:T(8,128)(2,1)S(1)} %cross_weights.3), channel_id=1, source_target_pairs={{0,8},{4,12},{1,9},{5,13},{2,10},{6,14},{3,11},{7,15},{16,24},{20,... | collective-permute-start | bytes 1867784 | tf_op jit(solution)/shard_map/ppermute | solution.py:578
  48.5 6.3 %row_attention.3.refs_0_ = f32[8,256,256]{2,1,0:T(8,128)S(1)} custom-call(s32[3]{0:T(128)S(1)} %pad_add_fusion.info, bf16[2,256,256]{2,1,0:T(8,128)(2,1)S(1)} %collective-permute-done.1.refs_0_.refs_1_, bf16[2,256,256]{2,1,0:T(8,128)(2,1)S(1)} %collective-permute-done.1.refs_0_.refs_1_, ...), custom_call_target="tpu_custom_call" | custom-call | flops 40000000000 | bytes 1 | tf_op jit(solution)/shard_map/row_attention/pallas_call | solution.py:146
  54.8 1.3 %collective-permute-done.5.qo_ref.vo_ref = bf16[64,16,256]{2,1,0:T(8,128)(2,1)S(1)} collective-permute-done((bf16[64,16,256]{2,1,0:T(8,128)(2,1)S(1)}, bf16[64,16,256]{2,1,0:T(8,128)(2,1)S(1)}, u32[]{:S(2)}, u32[]{:S(2)}) %collective-permute-start.5) | collective-permute-done | bytes 524320 | tf_op jit(solution)/shard_map/ppermute | solution.py:578
  56.1 0.6 cross_weights.4
  56.7 1.3 %collective-permute-start.7 = (bf16[1216,128]{1,0:T(8,128)(2,1)S(1)}, bf16[1216,128]{1,0:T(8,128)(2,1)S(1)}, u32[]{:S(2)}, u32[]{:S(2)}) collective-permute-start(bf16[1216,128]{1,0:T(8,128)(2,1)S(1)} %cross_weights.4), channel_id=1, source_target_pairs={{0,8},{4,12},{1,9},{5,13},{2,10},{6,14},{3,11},{7,15},{16,24},{20,... | collective-permute-start | bytes 933896 | tf_op jit(solution)/shard_map/ppermute | solution.py:578
  58.0 0.6 cross_weights.5
  58.5 1.3 %collective-permute-start.9 = (bf16[1216,128]{1,0:T(8,128)(2,1)S(1)}, bf16[1216,128]{1,0:T(8,128)(2,1)S(1)}, u32[]{:S(2)}, u32[]{:S(2)}) collective-permute-start(bf16[1216,128]{1,0:T(8,128)(2,1)S(1)} %cross_weights.5), channel_id=1, source_target_pairs={{0,8},{4,12},{1,9},{5,13},{2,10},{6,14},{3,11},{7,15},{16,24},{20,... | collective-permute-start | bytes 933896 | tf_op jit(solution)/shard_map/ppermute | solution.py:578
  59.8 13.2 %collective-permute-done.6.w_ref = bf16[2432,128]{1,0:T(8,128)(2,1)S(1)} collective-permute-done((bf16[2432,128]{1,0:T(8,128)(2,1)S(1)}, bf16[2432,128]{1,0:T(8,128)(2,1)S(1)}, u32[]{:S(2)}, u32[]{:S(2)}) %collective-permute-start.6) | collective-permute-done | bytes 622624 | tf_op jit(solution)/shard_map/ppermute | solution.py:578
  73.1 6.0 %column_attention.3 = (bf16[64,16,256]{2,1,0:T(8,128)(2,1)S(1)}, bf16[64,16,256]{2,1,0:T(8,128)(2,1)S(1)}) custom-call(s32[3]{0:T(128)S(1)} %pad_add_fusion.info, bf16[3,128,16,256]{3,2,1,0:T(8,128)(2,1)S(1)} %get-tuple-element.47.mine_ref, bf16[3,128,16,256]{3,2,1,0:T(8,128)(2,1)S(1)} %collective-permute-done.2.other_ref, ...), custom_call_target="tpu_custom_call" | custom-call | flops 1 | bytes 1 | tf_op jit(solution)/shard_map/column_attention/pallas_call | solution.py:146
  79.0 0.4 collective-permute-start.8
  79.5 0.2 collective-permute-done.7.w_ref
  79.7 3.3 %column_attention.4 = (bf16[32,16,256]{2,1,0:T(8,128)(2,1)S(1)}, bf16[32,16,256]{2,1,0:T(8,128)(2,1)S(1)}) custom-call(s32[3]{0:T(128)S(1)} %pad_add_fusion.info, bf16[3,128,16,256]{3,2,1,0:T(8,128)(2,1)S(1)} %get-tuple-element.47.mine_ref, bf16[3,128,16,256]{3,2,1,0:T(8,128)(2,1)S(1)} %collective-permute-done.2.other_ref, ...), custom_call_target="tpu_custom_call" | custom-call | flops 40000000000 | bytes 1 | tf_op jit(solution)/shard_map/column_attention/pallas_call | solution.py:146
  83.0 0.4 collective-permute-start.10
  83.4 1.9 %mix.3.refs_4_ = bf16[16,256,256]{2,1,0:T(8,128)(2,1)} custom-call(s32[3]{0:T(128)S(1)} %pad_add_fusion.info, f32[8,256,256]{2,1,0:T(8,128)S(1)} %row_attention.3.refs_0_, f32[8,256,256]{2,1,0:T(8,128)S(1)} %row_attention.2.refs_1_, bf16[64,16,256]{2,1,0:T(8,128)(2,1)S(1)} %get-tuple-element.58.refs_2_, bf16[64,16,256]{2,1,0:T(8,128)(2,1)S(1)} %collective-permute-done.8.refs_3_), custom_call_target="tpu_custom_call" | custom-call | flops 1 | bytes 1 | tf_op jit(solution)/shard_map/mix/pallas_call | solution.py:146
  85.3 1.1 %collective-permute-done.9.w_ref = bf16[1216,128]{1,0:T(8,128)(2,1)S(1)} collective-permute-done((bf16[1216,128]{1,0:T(8,128)(2,1)S(1)}, bf16[1216,128]{1,0:T(8,128)(2,1)S(1)}, u32[]{:S(2)}, u32[]{:S(2)}) %collective-permute-start.9) | collective-permute-done | bytes 311328 | tf_op jit(solution)/shard_map/ppermute | solution.py:578
  86.4 3.3 %column_attention.5 = (bf16[32,16,256]{2,1,0:T(8,128)(2,1)S(1)}, bf16[32,16,256]{2,1,0:T(8,128)(2,1)S(1)}) custom-call(s32[3]{0:T(128)S(1)} %pad_add_fusion.info, bf16[3,128,16,256]{3,2,1,0:T(8,128)(2,1)S(1)} %get-tuple-element.47.mine_ref, bf16[3,128,16,256]{3,2,1,0:T(8,128)(2,1)S(1)} %collective-permute-done.2.other_ref, ...), custom_call_target="tpu_custom_call" | custom-call | flops 40000000000 | bytes 1 | tf_op jit(solution)/shard_map/column_attention/pallas_call | solution.py:146
  89.7 0.5 collective-permute-start.11
  90.1 1.5 %mix.4.refs_4_ = bf16[16,256,256]{2,1,0:T(8,128)(2,1)} custom-call(s32[3]{0:T(128)S(1)} %pad_add_fusion.info, f32[8,256,256]{2,1,0:T(8,128)S(1)} %row_attention.3.refs_0_, f32[8,256,256]{2,1,0:T(8,128)S(1)} %row_attention.2.refs_1_, bf16[32,16,256]{2,1,0:T(8,128)(2,1)S(1)} %get-tuple-element.60.refs_2_, ...), custom_call_target="tpu_custom_call", output_to_operand_aliasing={{}: (5, {})} | custom-call | flops 1 | bytes 1 | tf_op jit(solution)/shard_map/mix/pallas_call | solution.py:146
  91.6 1.5 %mix.5 = bf16[16,256,256]{2,1,0:T(8,128)(2,1)} custom-call(s32[3]{0:T(128)S(1)} %pad_add_fusion.info, f32[8,256,256]{2,1,0:T(8,128)S(1)} %row_attention.3.refs_0_, f32[8,256,256]{2,1,0:T(8,128)S(1)} %row_attention.2.refs_1_, bf16[32,16,256]{2,1,0:T(8,128)(2,1)S(1)} %get-tuple-element.64.refs_2_, ...), custom_call_target="tpu_custom_call", output_to_operand_aliasing={{}: (5, {})} | custom-call | flops 1 | bytes 1 | tf_op jit(solution)/shard_map/mix/pallas_call | solution.py:146
  (9 shorter events, 0.1 us)
Async XLA Ops:
  0.1 7.4 %copy-start = (bf16[1024,3,256]{2,0,1:T(8,128)(2,1)S(1)}, bf16[1024,3,256]{2,0,1:T(8,128)(2,1)}, u32[]{:S(2)}) copy-start(bf16[1024,3,256]{2,0,1:T(8,128)(2,1)} %param.3) | copy-start | bytes 4718596
  7.4 24.1 %collective-permute-start = (bf16[128,16,256]{2,1,0:T(8,128)(2,1)S(1)}, bf16[128,16,256]{2,1,0:T(8,128)(2,1)S(1)}, u32[]{:S(2)}, u32[]{:S(2)}) collective-permute-start(bf16[128,16,256]{2,1,0:T(8,128)(2,1)S(1)} %get-tuple-element.37), channel_id=1, source_target_pairs={{0,8},{4,12},{8,0},{12,4},{1,9},{5,13},{9,1},{13,5},{2,10},{6,14},... | collective-permute-start | bytes 3145736 | tf_op jit(solution)/shard_map/ppermute | solution.py:578
  14.2 4.4 %collective-permute-start.1 = (bf16[2,256,256]{2,1,0:T(8,128)(2,1)S(1)}, bf16[2,256,256]{2,1,0:T(8,128)(2,1)S(1)}, u32[]{:S(2)}, u32[]{:S(2)}) collective-permute-start(bf16[2,256,256]{2,1,0:T(8,128)(2,1)S(1)} %get-tuple-element.43), channel_id=1, source_target_pairs={{0,4},{4,8},{8,12},{1,5},{5,9},{9,13},{2,6},{6,10},{10,14},{3,7},{... | collective-permute-start | bytes 786440 | tf_op jit(solution)/shard_map/ppermute | solution.py:578
  15.5 29.7 %collective-permute-start.3 = (bf16[64,16,256]{2,1,0:T(8,128)(2,1)S(1)}, bf16[64,16,256]{2,1,0:T(8,128)(2,1)S(1)}, u32[]{:S(2)}, u32[]{:S(2)}) collective-permute-start(bf16[64,16,256]{2,1,0:T(8,128)(2,1)S(1)} %get-tuple-element.51), channel_id=1, source_target_pairs={{0,12},{4,8},{8,4},{12,0},{1,13},{5,9},{9,5},{13,1},{2,14},{6,10},... | collective-permute-start | bytes 1572872 | tf_op jit(solution)/shard_map/ppermute | solution.py:578
  18.1 19.7 %collective-permute-start.2 = (bf16[3,128,16,256]{3,2,1,0:T(8,128)(2,1)S(1)}, bf16[3,128,16,256]{3,2,1,0:T(8,128)(2,1)S(1)}, u32[]{:S(2)}, u32[]{:S(2)}) collective-permute-start(bf16[3,128,16,256]{3,2,1,0:T(8,128)(2,1)S(1)} %get-tuple-element.48), channel_id=1, source_target_pairs={{0,4},{4,0},{8,12},{12,8},{1,5},{5,1},{9,13},{13,9},{2,6},{6,2},{1... | collective-permute-start | bytes 9437192 | tf_op jit(solution)/shard_map/ppermute | solution.py:578
  42.1 4.4 %collective-permute-start.4 = (f32[128,128]{1,0:T(8,128)S(1)}, f32[128,128]{1,0:T(8,128)S(1)}, u32[]{:S(2)}, u32[]{:S(2)}) collective-permute-start(f32[128,128]{1,0:T(8,128)S(1)} %maxima.1), channel_id=1, source_target_pairs={{8,0},{12,4},{9,1},{13,5},{10,2},{14,6},{11,3},{15,7},{24,16},{28,... | collective-permute-start | bytes 196616 | tf_op jit(solution)/shard_map/ppermute | solution.py:578
  45.1 11.0 %collective-permute-start.5 = (bf16[64,16,256]{2,1,0:T(8,128)(2,1)S(1)}, bf16[64,16,256]{2,1,0:T(8,128)(2,1)S(1)}, u32[]{:S(2)}, u32[]{:S(2)}) collective-permute-start(bf16[64,16,256]{2,1,0:T(8,128)(2,1)S(1)} %get-tuple-element.55), channel_id=1, source_target_pairs={{0,12},{4,8},{8,4},{12,0},{1,13},{5,9},{9,5},{13,1},{2,14},{6,10},... | collective-permute-start | bytes 1572872 | tf_op jit(solution)/shard_map/ppermute | solution.py:578
  47.0 26.1 %collective-permute-start.6 = (bf16[2432,128]{1,0:T(8,128)(2,1)S(1)}, bf16[2432,128]{1,0:T(8,128)(2,1)S(1)}, u32[]{:S(2)}, u32[]{:S(2)}) collective-permute-start(bf16[2432,128]{1,0:T(8,128)(2,1)S(1)} %cross_weights.3), channel_id=1, source_target_pairs={{0,8},{4,12},{1,9},{5,13},{2,10},{6,14},{3,11},{7,15},{16,24},{20,... | collective-permute-start | bytes 1867784 | tf_op jit(solution)/shard_map/ppermute | solution.py:578
  56.7 23.1 %collective-permute-start.7 = (bf16[1216,128]{1,0:T(8,128)(2,1)S(1)}, bf16[1216,128]{1,0:T(8,128)(2,1)S(1)}, u32[]{:S(2)}, u32[]{:S(2)}) collective-permute-start(bf16[1216,128]{1,0:T(8,128)(2,1)S(1)} %cross_weights.4), channel_id=1, source_target_pairs={{0,8},{4,12},{1,9},{5,13},{2,10},{6,14},{3,11},{7,15},{16,24},{20,... | collective-permute-start | bytes 933896 | tf_op jit(solution)/shard_map/ppermute | solution.py:578
  58.5 27.9 %collective-permute-start.9 = (bf16[1216,128]{1,0:T(8,128)(2,1)S(1)}, bf16[1216,128]{1,0:T(8,128)(2,1)S(1)}, u32[]{:S(2)}, u32[]{:S(2)}) collective-permute-start(bf16[1216,128]{1,0:T(8,128)(2,1)S(1)} %cross_weights.5), channel_id=1, source_target_pairs={{0,8},{4,12},{1,9},{5,13},{2,10},{6,14},{3,11},{7,15},{16,24},{20,... | collective-permute-start | bytes 933896 | tf_op jit(solution)/shard_map/ppermute | solution.py:578
  79.0 4.4 %collective-permute-start.8 = (bf16[64,16,256]{2,1,0:T(8,128)(2,1)S(1)}, bf16[64,16,256]{2,1,0:T(8,128)(2,1)S(1)}, u32[]{:S(2)}, u32[]{:S(2)}) collective-permute-start(bf16[64,16,256]{2,1,0:T(8,128)(2,1)S(1)} %get-tuple-element.62), channel_id=1, source_target_pairs={{0,4},{4,0},{8,12},{12,8},{1,5},{5,1},{9,13},{13,9},{2,6},{6,2},{1... | collective-permute-start | bytes 1572872 | tf_op jit(solution)/shard_map/ppermute | solution.py:578
  83.0 7.1 %collective-permute-start.10 = (bf16[32,16,256]{2,1,0:T(8,128)(2,1)S(1)}, bf16[32,16,256]{2,1,0:T(8,128)(2,1)S(1)}, u32[]{:S(2)}, u32[]{:S(2)}) collective-permute-start(bf16[32,16,256]{2,1,0:T(8,128)(2,1)S(1)} %get-tuple-element.66), channel_id=1, source_target_pairs={{0,4},{4,0},{8,12},{12,8},{1,5},{5,1},{9,13},{13,9},{2,6},{6,2},{1... | collective-permute-start | bytes 786440 | tf_op jit(solution)/shard_map/ppermute | solution.py:578
  89.7 2.0 %collective-permute-start.11 = (bf16[32,16,256]{2,1,0:T(8,128)(2,1)S(1)}, bf16[32,16,256]{2,1,0:T(8,128)(2,1)S(1)}, u32[]{:S(2)}, u32[]{:S(2)}) collective-permute-start(bf16[32,16,256]{2,1,0:T(8,128)(2,1)S(1)} %get-tuple-element.68), channel_id=1, source_target_pairs={{0,4},{4,0},{8,12},{12,8},{1,5},{5,1},{9,13},{13,9},{2,6},{6,2},{1... | collective-permute-start | bytes 786440 | tf_op jit(solution)/shard_map/ppermute | solution.py:578

commit v2 on v1

--- a/solution.py
+++ b/solution.py
@@ -153,7 +153,7 @@
             **options,
         ),
         input_output_aliases=aliases,
-        compiler_params=pltpu.CompilerParams(vmem_limit_bytes=28 << 20),
+        compiler_params=pltpu.CompilerParams(vmem_limit_bytes=20 << 20),
         cost_estimate=pl.CostEstimate(flops=flops, bytes_accessed=1, transcendentals=0),
         name=name,
     )(info, *operands)
@@ -186,30 +186,27 @@
         ref[...] = turned
 
 
-def first_kernel(info, x_ref, w_ref, *refs, block):
-    natural_ref, mine_ref, other_ref, last_ref, send_mine_ref = refs[:5]
-    send_others, x_out, w_buf, x_sem, w_sem = refs[5:7], refs[7], *refs[8:]
+def sent_kernel(info, x_ref, w_ref, *refs, other, sends, block):
+    refs = refs[-7 - sends :]
+    natural_ref, last_ref, x_out, triple_ref = refs[:4]
+    send_refs, (w_buf, x_sem, w_sem) = refs[4:-3], refs[-3:]
     slot = sent_slot(info)
     w_copy = pltpu.make_async_copy(w_ref.at[slot], w_buf, w_sem)
     w_copy.start()
     pieces = []
-    for other in (False, True):
-        for first in range(0, HALF, block):
-            columns = column_span(info, other, first, block)
-            copy = pltpu.make_async_copy(
-                x_ref.at[:, columns, :], x_out.at[:, columns, :], x_sem.at[len(pieces)]
-            )
-            copy.start()
-            pieces.append((copy, other, first, columns))
+    for first in range(0, HALF, block):
+        columns = column_span(info, other, first, block)
+        copy = pltpu.make_async_copy(
+            x_ref.at[:, columns, :], x_out.at[:, columns, :], x_sem.at[len(pieces)]
+        )
+        copy.start()
+        pieces.append((copy, first, columns))
     w_copy.wait()
     w = w_buf[...]
-    for copy, other, first, columns in pieces:
+    each = HALF // sends
+    for copy, first, columns in pieces:
         copy.wait()
-        triple_ref = other_ref if other else mine_ref
-        if other:
-            send_ref = send_others[first // SPLIT].at[pl.ds(first % SPLIT, block)]
-        else:
-            send_ref = send_mine_ref.at[pl.ds(first, block)]
+        send_ref = send_refs[first // each].at[pl.ds(first % each, block)]
         projected(
             x_out[:, columns, :],
             w,
@@ -239,23 +236,22 @@
                 )
 
 
-def project(info, x, w, block=64):
+def project_sent(info, x, w, kept, other, sends, block=64):
     width = w.shape[2]
-    natural = jax.ShapeDtypeStruct((3, STRIP, COLS, width), BF16)
-    triple = jax.ShapeDtypeStruct((3, HALF, STRIP, width), BF16)
-    last = jax.ShapeDtypeStruct((2, COLS, width), BF16)
-    sends = [jax.ShapeDtypeStruct((n, STRIP, width), BF16) for n in (HALF, SPLIT, HALF - SPLIT)]
+    shared = [(3, STRIP, COLS, width), (2, COLS, width), x.shape]
+    own = [(3, HALF, STRIP, width)] + [(HALF // sends, STRIP, width)] * sends
     return call(
-        functools.partial(first_kernel, block=block),
+        functools.partial(sent_kernel, other=other, sends=sends, block=block),
         info,
-        [x, w],
-        [natural, triple, triple, last] + sends + [jax.ShapeDtypeStruct(x.shape, BF16)],
+        [x, w] + list(kept),
+        [jax.ShapeDtypeStruct(shape, BF16) for shape in shared + own],
         [
             pltpu.VMEM(w.shape[1:], BF16),
-            pltpu.SemaphoreType.DMA((COLS // block,)),
+            pltpu.SemaphoreType.DMA((HALF // block,)),
             pltpu.SemaphoreType.DMA,
         ],
-        in_specs=[ANYWHERE] * 2,
+        in_specs=[ANYWHERE] * 2 + [ON_CHIP] * len(kept),
+        aliases={3 + n: n for n in range(len(kept))},
         name="project_sent",
     )
 
@@ -365,7 +361,7 @@
         body(g, pl.ds(first + g * PACK, PACK))
         return carry
 
-    lax.fori_loop(0, count // PACK, run, 0, unroll=4)
+    lax.fori_loop(0, count // PACK, run, 0, unroll=8)
 
 
 def maxima_kernel(info, mine_ref, other_ref, out_ref, *, heads):
@@ -594,18 +590,21 @@
     x = patches.reshape(STRIP, COLS, D)
     w = jnp.transpose(w_qkv, (1, 0, 2))
 
-    first = project(info, in_hbm(x), in_hbm(w))
-    recv_mine = send(first[4], SAME_CORE)
-    natural, mine, other, last = project_rest(info, first[7], w, first[:4])
+    x, from_hbm = in_hbm(x), in_hbm(w)
+    *shared, mine, sent = project_sent(info, x, from_hbm, (), False, 1)
+    recv_mine = send(sent, SAME_CORE)
+    *shared, other, sent, sent_later = project_sent(info, x, from_hbm, shared, True, 2)
+    natural, last, x = shared
+    natural, mine, other, last = project_rest(info, x, w, (natural, mine, other, last))
     other = send(other, CORE_SWAP)
     halo = send(last, NEXT_STRIP)
-    recv_others = [send(after(first[5], last), OTHER_CORE)]
+    recv_others = [send(after(sent, last), OTHER_CORE)]
     info = after(info, recv_mine, halo)
-    rows_low = row_part(info, None, natural, 8, 8)
+    rows_low = row_part(info, None, natural, 12, 4)
     info = after(info, rows_low)
     top = maxima(info, mine, other)
     below = send(top, UP_SAME)
-    recv_others.append(send(after(first[6], top), OTHER_CORE))
+    recv_others.append(send(after(sent_later, top), OTHER_CORE))
     info = after(info, top)
     far = []
     for n, (at, cols) in enumerate(chunks):
@@ -616,7 +615,7 @@
         info = after(info, weights)
         far.append(send(weights, DOWN_SAME))
         if n == 0:
-            rows_top = row_part(info, halo, natural, 0, 8)
+            rows_top = row_part(info, halo, natural, 0, 12)
             info = after(info, rows_top)
     row_context = (rows_top, rows_low)
     pending = []

time: 93.6 us -> 88 us (0.940)
  waiting for transfers between devices: 29.9 us -> 25.9 us
  Pallas kernels: 50 us -> 48.7 us
    ppermute x12, waiting for transfers between devices: 29.9 us -> 25.9 us  [send(): lax.ppermute(block, 'seq', route)]
    pallas_call x14 -> x15, Pallas kernels: 50 us -> 48.7 us  [call(): pl.pallas_call(kernel, out_shape=out_shape, grid_spec=pltpu.PrefetchScala...]
  transfers between devices with their start and end apart: 12 -> 12, of which waited for: 6 -> 4; matrix products, arithmetic and copies ran while one was open for 0% -> 0% of each run, Pallas kernels for 44% -> 49%
where the time goes in v2:
time: 88 us; the launch traced here: 87.8 us
  Pallas kernels  48.7 us (55%)
  waiting for transfers between devices  25.9 us (29%)
  starting transfers between devices  12.8 us (15%)
    pallas_call x15, Pallas kernels, call(): pl.pallas_call(kernel, out_shape=out_shape, grid_spec=pltpu.PrefetchScala...  48.7 us
    ppermute x12, waiting for transfers between devices, send(): lax.ppermute(block, 'seq', route)  25.9 us
    ppermute x12, starting transfers between devices, send(): lax.ppermute(block, 'seq', route)  12.8 us
  transfers between devices with their start and end apart: 12, of which 4 were waited for; matrix products, arithmetic and copies ran while one was open for 0% of the time, Pallas kernels for 49%

profile of v2, /device:TPU:5, one launch (start us, length us, event | category | flops | bytes accessed | tf_op | source)
XLA Modules:
  0.0 87.8 jit_solution(6201586366838082909)
XLA Ops:
  0.0 0.1 pad_add_fusion.info
  0.1 4.0 %project_sent.2 = (bf16[3,16,256,256]{3,2,1,0:T(8,128)(2,1)S(1)}, bf16[2,256,256]{2,1,0:T(8,128)(2,1)S(1)}, bf16[16,256,1024]{2,1,0:T(8,128)(2,1)S(1)}, bf16[3,1...) custom-call(s32[3]{0:T(128)S(1)} %pad_add_fusion.info, bf16[16,256,1024]{2,1,0:T(8,128)(2,1)} %bitcast.9, ...), custom_call_target="tpu_custom_call" | custom-call | flops 1 | bytes 1 | tf_op jit(solution)/shard_map/project_sent/pallas_call | solution.py:146
  4.1 0.1 collective-permute-start
  4.2 4.3 %project_sent.3 = (bf16[3,16,256,256]{3,2,1,0:T(8,128)(2,1)S(1)}, bf16[2,256,256]{2,1,0:T(8,128)(2,1)S(1)}, bf16[16,256,1024]{2,1,0:T(8,128)(2,1)S(1)}, bf16[3,1...) custom-call(s32[3]{0:T(128)S(1)} %pad_add_fusion.info, ...), custom_call_target="tpu_custom_call", output_to_operand_aliasing={{0}: (3, {}), {1}: (4, {}), {2}: (5, {})} | custom-call | flops 1 | bytes 1 | tf_op jit(solution)/shard_map/project_sent/pallas_call | solution.py:146
  8.5 6.8 %project_rest.1 = (bf16[3,16,256,256]{3,2,1,0:T(8,128)(2,1)S(1)}, bf16[3,128,16,256]{3,2,1,0:T(8,128)(2,1)S(1)}, bf16[3,128,16,256]{3,2,1,0:T(8,128)(2,1)S(1)}, bf16[2,256,256]{2,1,0:T(8,128)(2,1)S(1)}) custom-call(s32[3]{0:T(128)S(1)} %pad_add_fusion.info, ...), custom_call_target="tpu_custom_call", output_to_operand_aliasing={{0}: (3, {}), {1}: (4, {}), {2}: (5, {}), {3}: (6, {})} | custom-call | flops 1 | bytes 1 | tf_op jit(solution)/shard_map/project_rest/pallas_call | solution.py:146
  15.3 1.3 %collective-permute-start.1 = (bf16[2,256,256]{2,1,0:T(8,128)(2,1)S(1)}, bf16[2,256,256]{2,1,0:T(8,128)(2,1)S(1)}, u32[]{:S(2)}, u32[]{:S(2)}) collective-permute-start(bf16[2,256,256]{2,1,0:T(8,128)(2,1)S(1)} %get-tuple-element.49), channel_id=1, source_target_pairs={{0,4},{4,8},{8,12},{1,5},{5,9},{9,13},{2,6},{6,10},{10,14},{3,7},{... | collective-permute-start | bytes 786440 | tf_op jit(solution)/shard_map/ppermute | solution.py:574
  16.6 2.2 %collective-permute-start.3 = (bf16[64,16,256]{2,1,0:T(8,128)(2,1)S(1)}, bf16[64,16,256]{2,1,0:T(8,128)(2,1)S(1)}, u32[]{:S(2)}, u32[]{:S(2)}) collective-permute-start(bf16[64,16,256]{2,1,0:T(8,128)(2,1)S(1)} %get-tuple-element.57), channel_id=1, source_target_pairs={{0,12},{4,8},{8,4},{12,0},{1,13},{5,9},{9,5},{13,1},{2,14},{6,10},... | collective-permute-start | bytes 1572872 | tf_op jit(solution)/shard_map/ppermute | solution.py:574
  18.8 0.9 collective-permute-start.2
  19.7 8.5 %collective-permute-done.qm_ref.vm_ref = bf16[128,16,256]{2,1,0:T(8,128)(2,1)S(1)} collective-permute-done((bf16[128,16,256]{2,1,0:T(8,128)(2,1)S(1)}, bf16[128,16,256]{2,1,0:T(8,128)(2,1)S(1)}, u32[]{:S(2)}, u32[]{:S(2)}) %collective-permute-start) | collective-permute-done | bytes 1048608 | tf_op jit(solution)/shard_map/ppermute | solution.py:574
  28.2 3.4 %row_attention.2.refs_1_ = f32[4,256,256]{2,1,0:T(8,128)S(1)} custom-call(s32[3]{0:T(128)S(1)} %pad_add_fusion.info, bf16[3,16,256,256]{3,2,1,0:T(8,128)(2,1)S(1)} %get-tuple-element.51.refs_0_.refs_1_.refs_2_.refs_3_.refs_4_, bf16[3,16,256,256]{3,2,1,0:T(8,128)(2,1)S(1)} %get-tuple-element.51.refs_0_.refs_1_.refs_2_.refs_3_.refs_4_, ...), custom_call_target="tpu_custom_call" | custom-call | flops 40000000000 | bytes 1 | tf_op jit(solution)/shard_map/row_attention/pallas_call | solution.py:146
  31.6 3.9 %maxima.1 = f32[128,128]{1,0:T(8,128)S(1)} custom-call(s32[3]{0:T(128)S(1)} %pad_add_fusion.info, bf16[3,128,16,256]{3,2,1,0:T(8,128)(2,1)S(1)} %get-tuple-element.53.mine_ref, bf16[3,128,16,256]{3,2,1,0:T(8,128)(2,1)S(1)} %collective-permute-done.2.other_ref), custom_call_target="tpu_custom_call" | custom-call | flops 1 | bytes 1 | tf_op jit(solution)/shard_map/maxima/pallas_call | solution.py:146
  35.5 3.5 %collective-permute-start.4 = (f32[128,128]{1,0:T(8,128)S(1)}, f32[128,128]{1,0:T(8,128)S(1)}, u32[]{:S(2)}, u32[]{:S(2)}) collective-permute-start(f32[128,128]{1,0:T(8,128)S(1)} %maxima.1), channel_id=1, source_target_pairs={{8,0},{12,4},{9,1},{13,5},{10,2},{14,6},{11,3},{15,7},{24,16},{28,... | collective-permute-start | bytes 196616 | tf_op jit(solution)/shard_map/ppermute | solution.py:574
  39.0 0.1 collective-permute-start.5
  39.1 2.6 %collective-permute-done.3.qo_ref.vo_ref = bf16[64,16,256]{2,1,0:T(8,128)(2,1)S(1)} collective-permute-done((bf16[64,16,256]{2,1,0:T(8,128)(2,1)S(1)}, bf16[64,16,256]{2,1,0:T(8,128)(2,1)S(1)}, u32[]{:S(2)}, u32[]{:S(2)}) %collective-permute-start.3) | collective-permute-done | bytes 524320 | tf_op jit(solution)/shard_map/ppermute | solution.py:574
  41.7 0.6 cross_weights.3
  42.3 1.5 %collective-permute-start.6 = (bf16[2432,128]{1,0:T(8,128)(2,1)S(1)}, bf16[2432,128]{1,0:T(8,128)(2,1)S(1)}, u32[]{:S(2)}, u32[]{:S(2)}) collective-permute-start(bf16[2432,128]{1,0:T(8,128)(2,1)S(1)} %cross_weights.3), channel_id=1, source_target_pairs={{0,8},{4,12},{1,9},{5,13},{2,10},{6,14},{3,11},{7,15},{16,24},{20,... | collective-permute-start | bytes 1867784 | tf_op jit(solution)/shard_map/ppermute | solution.py:574
  43.8 9.2 %row_attention.3.refs_0_ = f32[12,256,256]{2,1,0:T(8,128)S(1)} custom-call(s32[3]{0:T(128)S(1)} %pad_add_fusion.info, bf16[2,256,256]{2,1,0:T(8,128)(2,1)S(1)} %collective-permute-done.1.refs_0_.refs_1_, bf16[2,256,256]{2,1,0:T(8,128)(2,1)S(1)} %collective-permute-done.1.refs_0_.refs_1_, ...), custom_call_target="tpu_custom_call" | custom-call | flops 40000000000 | bytes 1 | tf_op jit(solution)/shard_map/row_attention/pallas_call | solution.py:146
  52.9 0.6 cross_weights.4
  53.5 1.3 %collective-permute-start.7 = (bf16[1216,128]{1,0:T(8,128)(2,1)S(1)}, bf16[1216,128]{1,0:T(8,128)(2,1)S(1)}, u32[]{:S(2)}, u32[]{:S(2)}) collective-permute-start(bf16[1216,128]{1,0:T(8,128)(2,1)S(1)} %cross_weights.4), channel_id=1, source_target_pairs={{0,8},{4,12},{1,9},{5,13},{2,10},{6,14},{3,11},{7,15},{16,24},{20,... | collective-permute-start | bytes 933896 | tf_op jit(solution)/shard_map/ppermute | solution.py:574
  54.8 0.6 cross_weights.5
  55.4 1.3 %collective-permute-start.9 = (bf16[1216,128]{1,0:T(8,128)(2,1)S(1)}, bf16[1216,128]{1,0:T(8,128)(2,1)S(1)}, u32[]{:S(2)}, u32[]{:S(2)}) collective-permute-start(bf16[1216,128]{1,0:T(8,128)(2,1)S(1)} %cross_weights.5), channel_id=1, source_target_pairs={{0,8},{4,12},{1,9},{5,13},{2,10},{6,14},{3,11},{7,15},{16,24},{20,... | collective-permute-start | bytes 933896 | tf_op jit(solution)/shard_map/ppermute | solution.py:574
  56.7 13.1 %collective-permute-done.6.w_ref = bf16[2432,128]{1,0:T(8,128)(2,1)S(1)} collective-permute-done((bf16[2432,128]{1,0:T(8,128)(2,1)S(1)}, bf16[2432,128]{1,0:T(8,128)(2,1)S(1)}, u32[]{:S(2)}, u32[]{:S(2)}) %collective-permute-start.6) | collective-permute-done | bytes 622624 | tf_op jit(solution)/shard_map/ppermute | solution.py:574
  69.8 5.1 %column_attention.3 = (bf16[64,16,256]{2,1,0:T(8,128)(2,1)S(1)}, bf16[64,16,256]{2,1,0:T(8,128)(2,1)S(1)}) custom-call(s32[3]{0:T(128)S(1)} %pad_add_fusion.info, bf16[3,128,16,256]{3,2,1,0:T(8,128)(2,1)S(1)} %get-tuple-element.53.mine_ref, bf16[3,128,16,256]{3,2,1,0:T(8,128)(2,1)S(1)} %collective-permute-done.2.other_ref, ...), custom_call_target="tpu_custom_call" | custom-call | flops 1 | bytes 1 | tf_op jit(solution)/shard_map/column_attention/pallas_call | solution.py:146
  74.9 0.1 collective-permute-start.8
  75.0 1.5 %collective-permute-done.7.w_ref = bf16[1216,128]{1,0:T(8,128)(2,1)S(1)} collective-permute-done((bf16[1216,128]{1,0:T(8,128)(2,1)S(1)}, bf16[1216,128]{1,0:T(8,128)(2,1)S(1)}, u32[]{:S(2)}, u32[]{:S(2)}) %collective-permute-start.7) | collective-permute-done | bytes 311328 | tf_op jit(solution)/shard_map/ppermute | solution.py:574
  76.5 2.8 %column_attention.4 = (bf16[32,16,256]{2,1,0:T(8,128)(2,1)S(1)}, bf16[32,16,256]{2,1,0:T(8,128)(2,1)S(1)}) custom-call(s32[3]{0:T(128)S(1)} %pad_add_fusion.info, bf16[3,128,16,256]{3,2,1,0:T(8,128)(2,1)S(1)} %get-tuple-element.53.mine_ref, bf16[3,128,16,256]{3,2,1,0:T(8,128)(2,1)S(1)} %collective-permute-done.2.other_ref, ...), custom_call_target="tpu_custom_call" | custom-call | flops 40000000000 | bytes 1 | tf_op jit(solution)/shard_map/column_attention/pallas_call | solution.py:146
  79.3 0.1 collective-permute-start.10
  79.4 1.9 %mix.3.refs_4_ = bf16[16,256,256]{2,1,0:T(8,128)(2,1)} custom-call(s32[3]{0:T(128)S(1)} %pad_add_fusion.info, f32[12,256,256]{2,1,0:T(8,128)S(1)} %row_attention.3.refs_0_, f32[4,256,256]{2,1,0:T(8,128)S(1)} %row_attention.2.refs_1_, bf16[64,16,256]{2,1,0:T(8,128)(2,1)S(1)} %get-tuple-element.64.refs_2_, bf16[64,16,256]{2,1,0:T(8,128)(2,1)S(1)} %collective-permute-done.8.refs_3_), custom_call_target="tpu_custom_call" | custom-call | flops 1 | bytes 1 | tf_op jit(solution)/shard_map/mix/pallas_call | solution.py:146
  81.3 2.8 %column_attention.5 = (bf16[32,16,256]{2,1,0:T(8,128)(2,1)S(1)}, bf16[32,16,256]{2,1,0:T(8,128)(2,1)S(1)}) custom-call(s32[3]{0:T(128)S(1)} %pad_add_fusion.info, bf16[3,128,16,256]{3,2,1,0:T(8,128)(2,1)S(1)} %get-tuple-element.53.mine_ref, bf16[3,128,16,256]{3,2,1,0:T(8,128)(2,1)S(1)} %collective-permute-done.2.other_ref, ...), custom_call_target="tpu_custom_call" | custom-call | flops 40000000000 | bytes 1 | tf_op jit(solution)/shard_map/column_attention/pallas_call | solution.py:146
  84.0 0.6 collective-permute-start.11
  84.6 1.5 %mix.4.refs_4_ = bf16[16,256,256]{2,1,0:T(8,128)(2,1)} custom-call(s32[3]{0:T(128)S(1)} %pad_add_fusion.info, f32[12,256,256]{2,1,0:T(8,128)S(1)} %row_attention.3.refs_0_, f32[4,256,256]{2,1,0:T(8,128)S(1)} %row_attention.2.refs_1_, bf16[32,16,256]{2,1,0:T(8,128)(2,1)S(1)} %get-tuple-element.66.refs_2_, ...), custom_call_target="tpu_custom_call", output_to_operand_aliasing={{}: (5, {})} | custom-call | flops 1 | bytes 1 | tf_op jit(solution)/shard_map/mix/pallas_call | solution.py:146
  86.1 1.5 %mix.5 = bf16[16,256,256]{2,1,0:T(8,128)(2,1)} custom-call(s32[3]{0:T(128)S(1)} %pad_add_fusion.info, f32[12,256,256]{2,1,0:T(8,128)S(1)} %row_attention.3.refs_0_, f32[4,256,256]{2,1,0:T(8,128)S(1)} %row_attention.2.refs_1_, bf16[32,16,256]{2,1,0:T(8,128)(2,1)S(1)} %get-tuple-element.70.refs_2_, ...), custom_call_target="tpu_custom_call", output_to_operand_aliasing={{}: (5, {})} | custom-call | flops 1 | bytes 1 | tf_op jit(solution)/shard_map/mix/pallas_call | solution.py:146
  (10 shorter events, 0.0 us)
Async XLA Ops:
  4.1 24.1 %collective-permute-start = (bf16[128,16,256]{2,1,0:T(8,128)(2,1)S(1)}, bf16[128,16,256]{2,1,0:T(8,128)(2,1)S(1)}, u32[]{:S(2)}, u32[]{:S(2)}) collective-permute-start(bf16[128,16,256]{2,1,0:T(8,128)(2,1)S(1)} %get-tuple-element.40), channel_id=1, source_target_pairs={{0,8},{4,12},{8,0},{12,4},{1,9},{5,13},{9,1},{13,5},{2,10},{6,14},... | collective-permute-start | bytes 3145736 | tf_op jit(solution)/shard_map/ppermute | solution.py:574
  4.2 4.3 %copy-start = (bf16[1024,3,256]{2,0,1:T(8,128)(2,1)S(1)}, bf16[1024,3,256]{2,0,1:T(8,128)(2,1)}, u32[]{:S(2)}) copy-start(bf16[1024,3,256]{2,0,1:T(8,128)(2,1)} %param.3) | copy-start | bytes 4718596
  15.3 4.4 %collective-permute-start.1 = (bf16[2,256,256]{2,1,0:T(8,128)(2,1)S(1)}, bf16[2,256,256]{2,1,0:T(8,128)(2,1)S(1)}, u32[]{:S(2)}, u32[]{:S(2)}) collective-permute-start(bf16[2,256,256]{2,1,0:T(8,128)(2,1)S(1)} %get-tuple-element.49), channel_id=1, source_target_pairs={{0,4},{4,8},{8,12},{1,5},{5,9},{9,13},{2,6},{6,10},{10,14},{3,7},{... | collective-permute-start | bytes 786440 | tf_op jit(solution)/shard_map/ppermute | solution.py:574
  16.6 25.1 %collective-permute-start.3 = (bf16[64,16,256]{2,1,0:T(8,128)(2,1)S(1)}, bf16[64,16,256]{2,1,0:T(8,128)(2,1)S(1)}, u32[]{:S(2)}, u32[]{:S(2)}) collective-permute-start(bf16[64,16,256]{2,1,0:T(8,128)(2,1)S(1)} %get-tuple-element.57), channel_id=1, source_target_pairs={{0,12},{4,8},{8,4},{12,0},{1,13},{5,9},{9,5},{13,1},{2,14},{6,10},... | collective-permute-start | bytes 1572872 | tf_op jit(solution)/shard_map/ppermute | solution.py:574
  18.8 12.8 %collective-permute-start.2 = (bf16[3,128,16,256]{3,2,1,0:T(8,128)(2,1)S(1)}, bf16[3,128,16,256]{3,2,1,0:T(8,128)(2,1)S(1)}, u32[]{:S(2)}, u32[]{:S(2)}) collective-permute-start(bf16[3,128,16,256]{3,2,1,0:T(8,128)(2,1)S(1)} %get-tuple-element.54), channel_id=1, source_target_pairs={{0,4},{4,0},{8,12},{12,8},{1,5},{5,1},{9,13},{13,9},{2,6},{6,2},{1... | collective-permute-start | bytes 9437192 | tf_op jit(solution)/shard_map/ppermute | solution.py:574
  35.5 6.2 %collective-permute-start.4 = (f32[128,128]{1,0:T(8,128)S(1)}, f32[128,128]{1,0:T(8,128)S(1)}, u32[]{:S(2)}, u32[]{:S(2)}) collective-permute-start(f32[128,128]{1,0:T(8,128)S(1)} %maxima.1), channel_id=1, source_target_pairs={{8,0},{12,4},{9,1},{13,5},{10,2},{14,6},{11,3},{15,7},{24,16},{28,... | collective-permute-start | bytes 196616 | tf_op jit(solution)/shard_map/ppermute | solution.py:574
  39.0 14.0 %collective-permute-start.5 = (bf16[64,16,256]{2,1,0:T(8,128)(2,1)S(1)}, bf16[64,16,256]{2,1,0:T(8,128)(2,1)S(1)}, u32[]{:S(2)}, u32[]{:S(2)}) collective-permute-start(bf16[64,16,256]{2,1,0:T(8,128)(2,1)S(1)} %get-tuple-element.61), channel_id=1, source_target_pairs={{0,12},{4,8},{8,4},{12,0},{1,13},{5,9},{9,5},{13,1},{2,14},{6,10},... | collective-permute-start | bytes 1572872 | tf_op jit(solution)/shard_map/ppermute | solution.py:574
  42.3 27.5 %collective-permute-start.6 = (bf16[2432,128]{1,0:T(8,128)(2,1)S(1)}, bf16[2432,128]{1,0:T(8,128)(2,1)S(1)}, u32[]{:S(2)}, u32[]{:S(2)}) collective-permute-start(bf16[2432,128]{1,0:T(8,128)(2,1)S(1)} %cross_weights.3), channel_id=1, source_target_pairs={{0,8},{4,12},{1,9},{5,13},{2,10},{6,14},{3,11},{7,15},{16,24},{20,... | collective-permute-start | bytes 1867784 | tf_op jit(solution)/shard_map/ppermute | solution.py:574
  53.5 23.0 %collective-permute-start.7 = (bf16[1216,128]{1,0:T(8,128)(2,1)S(1)}, bf16[1216,128]{1,0:T(8,128)(2,1)S(1)}, u32[]{:S(2)}, u32[]{:S(2)}) collective-permute-start(bf16[1216,128]{1,0:T(8,128)(2,1)S(1)} %cross_weights.4), channel_id=1, source_target_pairs={{0,8},{4,12},{1,9},{5,13},{2,10},{6,14},{3,11},{7,15},{16,24},{20,... | collective-permute-start | bytes 933896 | tf_op jit(solution)/shard_map/ppermute | solution.py:574
  55.4 25.9 %collective-permute-start.9 = (bf16[1216,128]{1,0:T(8,128)(2,1)S(1)}, bf16[1216,128]{1,0:T(8,128)(2,1)S(1)}, u32[]{:S(2)}, u32[]{:S(2)}) collective-permute-start(bf16[1216,128]{1,0:T(8,128)(2,1)S(1)} %cross_weights.5), channel_id=1, source_target_pairs={{0,8},{4,12},{1,9},{5,13},{2,10},{6,14},{3,11},{7,15},{16,24},{20,... | collective-permute-start | bytes 933896 | tf_op jit(solution)/shard_map/ppermute | solution.py:574
  74.9 4.5 %collective-permute-start.8 = (bf16[64,16,256]{2,1,0:T(8,128)(2,1)S(1)}, bf16[64,16,256]{2,1,0:T(8,128)(2,1)S(1)}, u32[]{:S(2)}, u32[]{:S(2)}) collective-permute-start(bf16[64,16,256]{2,1,0:T(8,128)(2,1)S(1)} %get-tuple-element.68), channel_id=1, source_target_pairs={{0,4},{4,0},{8,12},{12,8},{1,5},{5,1},{9,13},{13,9},{2,6},{6,2},{1... | collective-permute-start | bytes 1572872 | tf_op jit(solution)/shard_map/ppermute | solution.py:574
  79.3 5.3 %collective-permute-start.10 = (bf16[32,16,256]{2,1,0:T(8,128)(2,1)S(1)}, bf16[32,16,256]{2,1,0:T(8,128)(2,1)S(1)}, u32[]{:S(2)}, u32[]{:S(2)}) collective-permute-start(bf16[32,16,256]{2,1,0:T(8,128)(2,1)S(1)} %get-tuple-element.72), channel_id=1, source_target_pairs={{0,4},{4,0},{8,12},{12,8},{1,5},{5,1},{9,13},{13,9},{2,6},{6,2},{1... | collective-permute-start | bytes 786440 | tf_op jit(solution)/shard_map/ppermute | solution.py:574
  84.0 2.1 %collective-permute-start.11 = (bf16[32,16,256]{2,1,0:T(8,128)(2,1)S(1)}, bf16[32,16,256]{2,1,0:T(8,128)(2,1)S(1)}, u32[]{:S(2)}, u32[]{:S(2)}) collective-permute-start(bf16[32,16,256]{2,1,0:T(8,128)(2,1)S(1)} %get-tuple-element.74), channel_id=1, source_target_pairs={{0,4},{4,0},{8,12},{12,8},{1,5},{5,1},{9,13},{13,9},{2,6},{6,2},{1... | collective-permute-start | bytes 786440 | tf_op jit(solution)/shard_map/ppermute | solution.py:574

commit v3 on v2

--- a/solution.py
+++ b/solution.py
@@ -186,7 +186,7 @@
         ref[...] = turned
 
 
-def sent_kernel(info, x_ref, w_ref, *refs, other, sends, block):
+def sent_kernel(info, x_ref, w_ref, *refs, other, start, cols, sends, block):
     refs = refs[-7 - sends :]
     natural_ref, last_ref, x_out, triple_ref = refs[:4]
     send_refs, (w_buf, x_sem, w_sem) = refs[4:-3], refs[-3:]
@@ -194,7 +194,7 @@
     w_copy = pltpu.make_async_copy(w_ref.at[slot], w_buf, w_sem)
     w_copy.start()
     pieces = []
-    for first in range(0, HALF, block):
+    for first in range(start, start + cols, block):
         columns = column_span(info, other, first, block)
         copy = pltpu.make_async_copy(
             x_ref.at[:, columns, :], x_out.at[:, columns, :], x_sem.at[len(pieces)]
@@ -203,10 +203,10 @@
         pieces.append((copy, first, columns))
     w_copy.wait()
     w = w_buf[...]
-    each = HALF // sends
+    each = cols // sends
     for copy, first, columns in pieces:
         copy.wait()
-        send_ref = send_refs[first // each].at[pl.ds(first % each, block)]
+        send_ref = send_refs[(first - start) // each].at[pl.ds((first - start) % each, block)]
         projected(
             x_out[:, columns, :],
             w,
@@ -236,18 +236,20 @@
                 )
 
 
-def project_sent(info, x, w, kept, other, sends, block=64):
+def project_sent(info, x, w, kept, other, start, cols, sends, block=64):
     width = w.shape[2]
     shared = [(3, STRIP, COLS, width), (2, COLS, width), x.shape]
-    own = [(3, HALF, STRIP, width)] + [(HALF // sends, STRIP, width)] * sends
+    own = [(3, HALF, STRIP, width)] + [(cols // sends, STRIP, width)] * sends
     return call(
-        functools.partial(sent_kernel, other=other, sends=sends, block=block),
+        functools.partial(
+            sent_kernel, other=other, start=start, cols=cols, sends=sends, block=block
+        ),
         info,
         [x, w] + list(kept),
         [jax.ShapeDtypeStruct(shape, BF16) for shape in shared + own],
         [
             pltpu.VMEM(w.shape[1:], BF16),
-            pltpu.SemaphoreType.DMA((HALF // block,)),
+            pltpu.SemaphoreType.DMA((cols // block,)),
             pltpu.SemaphoreType.DMA,
         ],
         in_specs=[ANYWHERE] * 2 + [ON_CHIP] * len(kept),
@@ -399,7 +401,8 @@
     spread = head_rows(BOTH, heads * HEAD_DIM)
 
     def body(g, part):
-        qm, qo = qm_ref[part], qo_ref[pl.ds(first - base + g * PACK, PACK)]
+        near = pl.ds(first - base + g * PACK, PACK)
+        qm, qo = qm_ref[near], qo_ref[near]
         km, ko = mine_ref[1, part], other_ref[1, part]
         below = top_ref[part]
         tops, totals, turned = [], [], []
@@ -476,7 +479,8 @@
         near = jnp.concatenate(turned, 0).T.astype(BF16)
         weights = jnp.concatenate([near, w_ref[pl.ds(g * rows, rows)]], 1)
         near_v = [column_of(mine_ref[2, part], other_ref[2, part], j) for j in range(PACK)]
-        vm, vo = vm_ref[part], vo_ref[pl.ds(first - base + g * PACK, PACK)]
+        sent = pl.ds(first - base + g * PACK, PACK)
+        vm, vo = vm_ref[sent], vo_ref[sent]
         far_v = [column_of(vm, vo, j) for j in range(PACK)]
         values = jnp.concatenate(near_v + far_v, 0)
         left = jnp.concatenate([weights * picks[j] for j in range(PACK)], 0)
@@ -584,22 +588,28 @@
 
 def two_chips(patches, w_qkv):
     width = w_qkv.shape[2]
-    chunks = ((0, 64), (64, 32), (96, 32))
+    chunks = ((0, 32), (32, 32), (64, 32), (96, 32))
     seq = lax.axis_index("seq")
     info = jnp.stack([seq % 2, seq // 2, seq]).astype(jnp.int32)
     x = patches.reshape(STRIP, COLS, D)
     w = jnp.transpose(w_qkv, (1, 0, 2))
 
     x, from_hbm = in_hbm(x), in_hbm(w)
-    *shared, mine, sent = project_sent(info, x, from_hbm, (), False, 1)
-    recv_mine = send(sent, SAME_CORE)
-    *shared, other, sent, sent_later = project_sent(info, x, from_hbm, shared, True, 2)
+    *shared, mine, sent = project_sent(info, x, from_hbm, (), False, 0, SPLIT, 1)
+    recv_mines = [send(sent, SAME_CORE)]
+    *shared, mine, sent = project_sent(
+        info, x, from_hbm, shared + [mine], False, SPLIT, HALF - SPLIT, 1
+    )
+    recv_mines.append(send(sent, SAME_CORE))
+    *shared, other, sent, sent_later = project_sent(
+        info, x, from_hbm, shared, True, 0, HALF, 2
+    )
     natural, last, x = shared
     natural, mine, other, last = project_rest(info, x, w, (natural, mine, other, last))
     other = send(other, CORE_SWAP)
     halo = send(last, NEXT_STRIP)
     recv_others = [send(after(sent, last), OTHER_CORE)]
-    info = after(info, recv_mine, halo)
+    info = after(info, *recv_mines, halo)
     rows_low = row_part(info, None, natural, 12, 4)
     info = after(info, rows_low)
     top = maxima(info, mine, other)
@@ -610,7 +620,7 @@
     for n, (at, cols) in enumerate(chunks):
         part = at // SPLIT
         weights = cross_weights(
-            info, recv_mine, recv_others[part], mine, other, below, at, cols, part * SPLIT
+            info, recv_mines[part], recv_others[part], mine, other, below, at, cols, part * SPLIT
         )
         info = after(info, weights)
         far.append(send(weights, DOWN_SAME))
@@ -626,7 +636,7 @@
             info,
             mine,
             other,
-            recv_mine,
+            recv_mines[part],
             recv_others[part],
             weights,
             at,

time: 88 us -> 91.9 us (1.044)
  waiting for transfers between devices: 25.9 us -> 11.8 us
  starting transfers between devices: 12.8 us -> 25.7 us
  Pallas kernels: 48.7 us -> 53.3 us
    ppermute x12 -> x15, waiting for transfers between devices: 25.9 us -> 11.8 us  [send(): lax.ppermute(block, 'seq', route)]
    ppermute x12 -> x15, starting transfers between devices: 12.8 us -> 25.7 us  [send(): lax.ppermute(block, 'seq', route)]
    pallas_call x15 -> x19, Pallas kernels: 48.7 us -> 53.3 us  [call(): pl.pallas_call(kernel, out_shape=out_shape, grid_spec=pltpu.PrefetchScala...]
  transfers between devices with their start and end apart: 12 -> 15, of which waited for: 4 -> 5; matrix products, arithmetic and copies ran while one was open for 0% -> 0% of each run, Pallas kernels for 49% -> 53%
where the time goes in v3:
time: 91.9 us; the launch traced here: 91.4 us
  Pallas kernels  53.3 us (58%)
  starting transfers between devices  25.7 us (28%)
  waiting for transfers between devices  11.8 us (13%)
    pallas_call x19, Pallas kernels, call(): pl.pallas_call(kernel, out_shape=out_shape, grid_spec=pltpu.PrefetchScala...  53.3 us
    ppermute x15, starting transfers between devices, send(): lax.ppermute(block, 'seq', route)  25.7 us
    ppermute x15, waiting for transfers between devices, send(): lax.ppermute(block, 'seq', route)  11.8 us
  transfers between devices with their start and end apart: 15, of which 5 were waited for; matrix products, arithmetic and copies ran while one was open for 0% of the time, Pallas kernels for 53%

profile of v3, /device:TPU:5, one launch (start us, length us, event | category | flops | bytes accessed | tf_op | source)
XLA Modules:
  0.0 91.4 jit_solution(2079020679722214969)
XLA Ops:
  0.1 3.2 %project_sent.3 = (bf16[3,16,256,256]{3,2,1,0:T(8,128)(2,1)S(1)}, bf16[2,256,256]{2,1,0:T(8,128)(2,1)S(1)}, bf16[16,256,1024]{2,1,0:T(8,128)(2,1)S(1)}, bf16[3,1...) custom-call(s32[3]{0:T(128)S(1)} %pad_add_fusion.info, bf16[16,256,1024]{2,1,0:T(8,128)(2,1)} %bitcast.10, ...), custom_call_target="tpu_custom_call" | custom-call | flops 1 | bytes 1 | tf_op jit(solution)/shard_map/project_sent/pallas_call | solution.py:146
  3.4 3.2 %project_sent.4 = (bf16[3,16,256,256]{3,2,1,0:T(8,128)(2,1)S(1)}, bf16[2,256,256]{2,1,0:T(8,128)(2,1)S(1)}, bf16[16,256,1024]{2,1,0:T(8,128)(2,1)S(1)}, bf16[3,1...) custom-call(s32[3]{0:T(128)S(1)} %pad_add_fusion.info, ...), custom_call_target="tpu_custom_call", output_to_operand_aliasing={{0}: (3, {}), {1}: (4, {}), {2}: (5, {}), {3}: (6, {})} | custom-call | flops 1 | bytes 1 | tf_op jit(solution)/shard_map/project_sent/pallas_call | solution.py:146
  6.6 1.5 %collective-permute-start.1 = (bf16[64,16,256]{2,1,0:T(8,128)(2,1)S(1)}, bf16[64,16,256]{2,1,0:T(8,128)(2,1)S(1)}, u32[]{:S(2)}, u32[]{:S(2)}) collective-permute-start(bf16[64,16,256]{2,1,0:T(8,128)(2,1)S(1)} %get-tuple-element.55), channel_id=1, source_target_pairs={{0,8},{4,12},{8,0},{12,4},{1,9},{5,13},{9,1},{13,5},{2,10},{6,14},... | collective-permute-start | bytes 1572872 | tf_op jit(solution)/shard_map/ppermute | solution.py:578
  8.1 4.3 %project_sent.5 = (bf16[3,16,256,256]{3,2,1,0:T(8,128)(2,1)S(1)}, bf16[2,256,256]{2,1,0:T(8,128)(2,1)S(1)}, bf16[16,256,1024]{2,1,0:T(8,128)(2,1)S(1)}, bf16[3,1...) custom-call(s32[3]{0:T(128)S(1)} %pad_add_fusion.info, ...), custom_call_target="tpu_custom_call", output_to_operand_aliasing={{0}: (3, {}), {1}: (4, {}), {2}: (5, {})} | custom-call | flops 1 | bytes 1 | tf_op jit(solution)/shard_map/project_sent/pallas_call | solution.py:146
  12.4 6.8 %project_rest.1 = (bf16[3,16,256,256]{3,2,1,0:T(8,128)(2,1)S(1)}, bf16[3,128,16,256]{3,2,1,0:T(8,128)(2,1)S(1)}, bf16[3,128,16,256]{3,2,1,0:T(8,128)(2,1)S(1)}, bf16[2,256,256]{2,1,0:T(8,128)(2,1)S(1)}) custom-call(s32[3]{0:T(128)S(1)} %pad_add_fusion.info, ...), custom_call_target="tpu_custom_call", output_to_operand_aliasing={{0}: (3, {}), {1}: (4, {}), {2}: (5, {}), {3}: (6, {})} | custom-call | flops 1 | bytes 1 | tf_op jit(solution)/shard_map/project_rest/pallas_call | solution.py:146
  19.2 1.3 %collective-permute-start.2 = (bf16[2,256,256]{2,1,0:T(8,128)(2,1)S(1)}, bf16[2,256,256]{2,1,0:T(8,128)(2,1)S(1)}, u32[]{:S(2)}, u32[]{:S(2)}) collective-permute-start(bf16[2,256,256]{2,1,0:T(8,128)(2,1)S(1)} %get-tuple-element.64), channel_id=1, source_target_pairs={{0,4},{4,8},{8,12},{1,5},{5,9},{9,13},{2,6},{6,10},{10,14},{3,7},{... | collective-permute-start | bytes 786440 | tf_op jit(solution)/shard_map/ppermute | solution.py:578
  20.5 0.8 collective-permute-start.4
  21.3 2.8 %collective-permute-start.3 = (bf16[3,128,16,256]{3,2,1,0:T(8,128)(2,1)S(1)}, bf16[3,128,16,256]{3,2,1,0:T(8,128)(2,1)S(1)}, u32[]{:S(2)}, u32[]{:S(2)}) collective-permute-start(bf16[3,128,16,256]{3,2,1,0:T(8,128)(2,1)S(1)} %get-tuple-element.69), channel_id=1, source_target_pairs={{0,4},{4,0},{8,12},{12,8},{1,5},{5,1},{9,13},{13,9},{2,6},{6,2},{1... | collective-permute-start | bytes 9437192 | tf_op jit(solution)/shard_map/ppermute | solution.py:578
  24.1 3.2 %collective-permute-done.1.qm_ref.vm_ref = bf16[64,16,256]{2,1,0:T(8,128)(2,1)S(1)} collective-permute-done((bf16[64,16,256]{2,1,0:T(8,128)(2,1)S(1)}, bf16[64,16,256]{2,1,0:T(8,128)(2,1)S(1)}, u32[]{:S(2)}, u32[]{:S(2)}) %collective-permute-start.1) | collective-permute-done | bytes 524320 | tf_op jit(solution)/shard_map/ppermute | solution.py:578
  27.4 3.4 %row_attention.2.refs_1_ = f32[4,256,256]{2,1,0:T(8,128)S(1)} custom-call(s32[3]{0:T(128)S(1)} %pad_add_fusion.info, bf16[3,16,256,256]{3,2,1,0:T(8,128)(2,1)S(1)} %get-tuple-element.66.refs_0_.refs_1_.refs_2_.refs_3_.refs_4_, bf16[3,16,256,256]{3,2,1,0:T(8,128)(2,1)S(1)} %get-tuple-element.66.refs_0_.refs_1_.refs_2_.refs_3_.refs_4_, ...), custom_call_target="tpu_custom_call" | custom-call | flops 40000000000 | bytes 1 | tf_op jit(solution)/shard_map/row_attention/pallas_call | solution.py:146
  30.8 3.9 %maxima.1 = f32[128,128]{1,0:T(8,128)S(1)} custom-call(s32[3]{0:T(128)S(1)} %pad_add_fusion.info, bf16[3,128,16,256]{3,2,1,0:T(8,128)(2,1)S(1)} %get-tuple-element.68.mine_ref, bf16[3,128,16,256]{3,2,1,0:T(8,128)(2,1)S(1)} %collective-permute-done.3.other_ref), custom_call_target="tpu_custom_call" | custom-call | flops 1 | bytes 1 | tf_op jit(solution)/shard_map/maxima/pallas_call | solution.py:146
  34.7 3.5 %collective-permute-start.5 = (f32[128,128]{1,0:T(8,128)S(1)}, f32[128,128]{1,0:T(8,128)S(1)}, u32[]{:S(2)}, u32[]{:S(2)}) collective-permute-start(f32[128,128]{1,0:T(8,128)S(1)} %maxima.1), channel_id=1, source_target_pairs={{8,0},{12,4},{9,1},{13,5},{10,2},{14,6},{11,3},{15,7},{24,16},{28,... | collective-permute-start | bytes 196616 | tf_op jit(solution)/shard_map/ppermute | solution.py:578
  38.3 2.6 %collective-permute-done.4.qo_ref.vo_ref = bf16[64,16,256]{2,1,0:T(8,128)(2,1)S(1)} collective-permute-done((bf16[64,16,256]{2,1,0:T(8,128)(2,1)S(1)}, bf16[64,16,256]{2,1,0:T(8,128)(2,1)S(1)}, u32[]{:S(2)}, u32[]{:S(2)}) %collective-permute-start.4) | collective-permute-done | bytes 524320 | tf_op jit(solution)/shard_map/ppermute | solution.py:578
  41.5 1.5 %collective-permute-start.7 = (bf16[1216,128]{1,0:T(8,128)(2,1)S(1)}, bf16[1216,128]{1,0:T(8,128)(2,1)S(1)}, u32[]{:S(2)}, u32[]{:S(2)}) collective-permute-start(bf16[1216,128]{1,0:T(8,128)(2,1)S(1)} %cross_weights.4), channel_id=1, source_target_pairs={{0,8},{4,12},{1,9},{5,13},{2,10},{6,14},{3,11},{7,15},{16,24},{20,... | collective-permute-start | bytes 933896 | tf_op jit(solution)/shard_map/ppermute | solution.py:578
  43.0 9.2 %row_attention.3.refs_0_ = f32[12,256,256]{2,1,0:T(8,128)S(1)} custom-call(s32[3]{0:T(128)S(1)} %pad_add_fusion.info, bf16[2,256,256]{2,1,0:T(8,128)(2,1)S(1)} %collective-permute-done.2.refs_0_.refs_1_, bf16[2,256,256]{2,1,0:T(8,128)(2,1)S(1)} %collective-permute-done.2.refs_0_.refs_1_, ...), custom_call_target="tpu_custom_call" | custom-call | flops 40000000000 | bytes 1 | tf_op jit(solution)/shard_map/row_attention/pallas_call | solution.py:146
  52.1 0.6 cross_weights.5
  52.7 1.3 %collective-permute-start.8 = (bf16[1216,128]{1,0:T(8,128)(2,1)S(1)}, bf16[1216,128]{1,0:T(8,128)(2,1)S(1)}, u32[]{:S(2)}, u32[]{:S(2)}) collective-permute-start(bf16[1216,128]{1,0:T(8,128)(2,1)S(1)} %cross_weights.5), channel_id=1, source_target_pairs={{0,8},{4,12},{1,9},{5,13},{2,10},{6,14},{3,11},{7,15},{16,24},{20,... | collective-permute-start | bytes 933896 | tf_op jit(solution)/shard_map/ppermute | solution.py:578
  55.1 1.3 %collective-permute-start.12 = (bf16[1216,128]{1,0:T(8,128)(2,1)S(1)}, bf16[1216,128]{1,0:T(8,128)(2,1)S(1)}, u32[]{:S(2)}, u32[]{:S(2)}) collective-permute-start(bf16[1216,128]{1,0:T(8,128)(2,1)S(1)} %cross_weights.7), channel_id=1, source_target_pairs={{0,8},{4,12},{1,9},{5,13},{2,10},{6,14},{3,11},{7,15},{16,24},{20,... | collective-permute-start | bytes 933896 | tf_op jit(solution)/shard_map/ppermute | solution.py:578
  56.4 1.3 %collective-permute-start.10 = (bf16[1216,128]{1,0:T(8,128)(2,1)S(1)}, bf16[1216,128]{1,0:T(8,128)(2,1)S(1)}, u32[]{:S(2)}, u32[]{:S(2)}) collective-permute-start(bf16[1216,128]{1,0:T(8,128)(2,1)S(1)} %cross_weights.6), channel_id=1, source_target_pairs={{0,8},{4,12},{1,9},{5,13},{2,10},{6,14},{3,11},{7,15},{16,24},{20,... | collective-permute-start | bytes 933896 | tf_op jit(solution)/shard_map/ppermute | solution.py:578
  57.7 2.4 %collective-permute-done.7.w_ref = bf16[1216,128]{1,0:T(8,128)(2,1)S(1)} collective-permute-done((bf16[1216,128]{1,0:T(8,128)(2,1)S(1)}, bf16[1216,128]{1,0:T(8,128)(2,1)S(1)}, u32[]{:S(2)}, u32[]{:S(2)}) %collective-permute-start.7) | collective-permute-done | bytes 311328 | tf_op jit(solution)/shard_map/ppermute | solution.py:578
  60.2 2.8 %column_attention.4 = (bf16[32,16,256]{2,1,0:T(8,128)(2,1)S(1)}, bf16[32,16,256]{2,1,0:T(8,128)(2,1)S(1)}) custom-call(s32[3]{0:T(128)S(1)} %pad_add_fusion.info, bf16[3,128,16,256]{3,2,1,0:T(8,128)(2,1)S(1)} %get-tuple-element.68.mine_ref, bf16[3,128,16,256]{3,2,1,0:T(8,128)(2,1)S(1)} %collective-permute-done.3.other_ref, ...), custom_call_target="tpu_custom_call" | custom-call | flops 1 | bytes 1 | tf_op jit(solution)/shard_map/column_attention/pallas_call | solution.py:146
  63.0 1.3 %collective-permute-start.9 = (bf16[32,16,256]{2,1,0:T(8,128)(2,1)S(1)}, bf16[32,16,256]{2,1,0:T(8,128)(2,1)S(1)}, u32[]{:S(2)}, u32[]{:S(2)}) collective-permute-start(bf16[32,16,256]{2,1,0:T(8,128)(2,1)S(1)} %get-tuple-element.84), channel_id=1, source_target_pairs={{0,4},{4,0},{8,12},{12,8},{1,5},{5,1},{9,13},{13,9},{2,6},{6,2},{1... | collective-permute-start | bytes 786440 | tf_op jit(solution)/shard_map/ppermute | solution.py:578
  64.5 2.8 %column_attention.5 = (bf16[32,16,256]{2,1,0:T(8,128)(2,1)S(1)}, bf16[32,16,256]{2,1,0:T(8,128)(2,1)S(1)}) custom-call(s32[3]{0:T(128)S(1)} %pad_add_fusion.info, bf16[3,128,16,256]{3,2,1,0:T(8,128)(2,1)S(1)} %get-tuple-element.68.mine_ref, bf16[3,128,16,256]{3,2,1,0:T(8,128)(2,1)S(1)} %collective-permute-done.3.other_ref, ...), custom_call_target="tpu_custom_call" | custom-call | flops 40000000000 | bytes 1 | tf_op jit(solution)/shard_map/column_attention/pallas_call | solution.py:146
  67.3 5.8 %collective-permute-start.11 = (bf16[32,16,256]{2,1,0:T(8,128)(2,1)S(1)}, bf16[32,16,256]{2,1,0:T(8,128)(2,1)S(1)}, u32[]{:S(2)}, u32[]{:S(2)}) collective-permute-start(bf16[32,16,256]{2,1,0:T(8,128)(2,1)S(1)} %get-tuple-element.88), channel_id=1, source_target_pairs={{0,4},{4,0},{8,12},{12,8},{1,5},{5,1},{9,13},{13,9},{2,6},{6,2},{1... | collective-permute-start | bytes 786440 | tf_op jit(solution)/shard_map/ppermute | solution.py:578
  73.1 1.5 %mix.4.refs_4_ = bf16[16,256,256]{2,1,0:T(8,128)(2,1)} custom-call(s32[3]{0:T(128)S(1)} %pad_add_fusion.info, f32[12,256,256]{2,1,0:T(8,128)S(1)} %row_attention.3.refs_0_, f32[4,256,256]{2,1,0:T(8,128)S(1)} %row_attention.2.refs_1_, bf16[32,16,256]{2,1,0:T(8,128)(2,1)S(1)} %get-tuple-element.80.refs_2_, bf16[32,16,256]{2,1,0:T(8,128)(2,1)S(1)} %collective-permute-done.9.refs_3_), custom_call_target="tpu_custom_call" | custom-call | flops 1 | bytes 1 | tf_op jit(solution)/shard_map/mix/pallas_call | solution.py:146
  74.6 3.2 %collective-permute-done.10.w_ref = bf16[1216,128]{1,0:T(8,128)(2,1)S(1)} collective-permute-done((bf16[1216,128]{1,0:T(8,128)(2,1)S(1)}, bf16[1216,128]{1,0:T(8,128)(2,1)S(1)}, u32[]{:S(2)}, u32[]{:S(2)}) %collective-permute-start.10) | collective-permute-done | bytes 311328 | tf_op jit(solution)/shard_map/ppermute | solution.py:578
  77.8 2.8 %column_attention.6 = (bf16[32,16,256]{2,1,0:T(8,128)(2,1)S(1)}, bf16[32,16,256]{2,1,0:T(8,128)(2,1)S(1)}) custom-call(s32[3]{0:T(128)S(1)} %pad_add_fusion.info, bf16[3,128,16,256]{3,2,1,0:T(8,128)(2,1)S(1)} %get-tuple-element.68.mine_ref, bf16[3,128,16,256]{3,2,1,0:T(8,128)(2,1)S(1)} %collective-permute-done.3.other_ref, ...), custom_call_target="tpu_custom_call" | custom-call | flops 40000000000 | bytes 1 | tf_op jit(solution)/shard_map/column_attention/pallas_call | solution.py:146
  80.6 1.5 %mix.5.refs_4_ = bf16[16,256,256]{2,1,0:T(8,128)(2,1)} custom-call(s32[3]{0:T(128)S(1)} %pad_add_fusion.info, f32[12,256,256]{2,1,0:T(8,128)S(1)} %row_attention.3.refs_0_, f32[4,256,256]{2,1,0:T(8,128)S(1)} %row_attention.2.refs_1_, bf16[32,16,256]{2,1,0:T(8,128)(2,1)S(1)} %get-tuple-element.82.refs_2_, ...), custom_call_target="tpu_custom_call", output_to_operand_aliasing={{}: (5, {})} | custom-call | flops 1 | bytes 1 | tf_op jit(solution)/shard_map/mix/pallas_call | solution.py:146
  82.1 3.1 %collective-permute-start.13 = (bf16[32,16,256]{2,1,0:T(8,128)(2,1)S(1)}, bf16[32,16,256]{2,1,0:T(8,128)(2,1)S(1)}, u32[]{:S(2)}, u32[]{:S(2)}) collective-permute-start(bf16[32,16,256]{2,1,0:T(8,128)(2,1)S(1)} %get-tuple-element.92), channel_id=1, source_target_pairs={{0,4},{4,0},{8,12},{12,8},{1,5},{5,1},{9,13},{13,9},{2,6},{6,2},{1... | collective-permute-start | bytes 786440 | tf_op jit(solution)/shard_map/ppermute | solution.py:578
  85.3 2.8 %column_attention.7 = (bf16[32,16,256]{2,1,0:T(8,128)(2,1)S(1)}, bf16[32,16,256]{2,1,0:T(8,128)(2,1)S(1)}) custom-call(s32[3]{0:T(128)S(1)} %pad_add_fusion.info, bf16[3,128,16,256]{3,2,1,0:T(8,128)(2,1)S(1)} %get-tuple-element.68.mine_ref, bf16[3,128,16,256]{3,2,1,0:T(8,128)(2,1)S(1)} %collective-permute-done.3.other_ref, ...), custom_call_target="tpu_custom_call" | custom-call | flops 40000000000 | bytes 1 | tf_op jit(solution)/shard_map/column_attention/pallas_call | solution.py:146
  88.2 1.5 %mix.6.refs_4_ = bf16[16,256,256]{2,1,0:T(8,128)(2,1)} custom-call(s32[3]{0:T(128)S(1)} %pad_add_fusion.info, f32[12,256,256]{2,1,0:T(8,128)S(1)} %row_attention.3.refs_0_, f32[4,256,256]{2,1,0:T(8,128)S(1)} %row_attention.2.refs_1_, bf16[32,16,256]{2,1,0:T(8,128)(2,1)S(1)} %get-tuple-element.86.refs_2_, ...), custom_call_target="tpu_custom_call", output_to_operand_aliasing={{}: (5, {})} | custom-call | flops 1 | bytes 1 | tf_op jit(solution)/shard_map/mix/pallas_call | solution.py:146
  89.7 1.5 %mix.7 = bf16[16,256,256]{2,1,0:T(8,128)(2,1)} custom-call(s32[3]{0:T(128)S(1)} %pad_add_fusion.info, f32[12,256,256]{2,1,0:T(8,128)S(1)} %row_attention.3.refs_0_, f32[4,256,256]{2,1,0:T(8,128)S(1)} %row_attention.2.refs_1_, bf16[32,16,256]{2,1,0:T(8,128)(2,1)S(1)} %get-tuple-element.90.refs_2_, ...), custom_call_target="tpu_custom_call", output_to_operand_aliasing={{}: (5, {})} | custom-call | flops 1 | bytes 1 | tf_op jit(solution)/shard_map/mix/pallas_call | solution.py:146
  (20 shorter events, 2.3 us)
Async XLA Ops:
  3.3 20.9 %collective-permute-start = (bf16[64,16,256]{2,1,0:T(8,128)(2,1)S(1)}, bf16[64,16,256]{2,1,0:T(8,128)(2,1)S(1)}, u32[]{:S(2)}, u32[]{:S(2)}) collective-permute-start(bf16[64,16,256]{2,1,0:T(8,128)(2,1)S(1)} %get-tuple-element.50), channel_id=1, source_target_pairs={{0,8},{4,12},{8,0},{12,4},{1,9},{5,13},{9,1},{13,5},{2,10},{6,14},... | collective-permute-start | bytes 1572872 | tf_op jit(solution)/shard_map/ppermute | solution.py:578
  6.6 20.8 %collective-permute-start.1 = (bf16[64,16,256]{2,1,0:T(8,128)(2,1)S(1)}, bf16[64,16,256]{2,1,0:T(8,128)(2,1)S(1)}, u32[]{:S(2)}, u32[]{:S(2)}) collective-permute-start(bf16[64,16,256]{2,1,0:T(8,128)(2,1)S(1)} %get-tuple-element.55), channel_id=1, source_target_pairs={{0,8},{4,12},{8,0},{12,4},{1,9},{5,13},{9,1},{13,5},{2,10},{6,14},... | collective-permute-start | bytes 1572872 | tf_op jit(solution)/shard_map/ppermute | solution.py:578
  8.1 4.3 %copy-start = (bf16[1024,3,256]{2,0,1:T(8,128)(2,1)S(1)}, bf16[1024,3,256]{2,0,1:T(8,128)(2,1)}, u32[]{:S(2)}) copy-start(bf16[1024,3,256]{2,0,1:T(8,128)(2,1)} %param.3) | copy-start | bytes 4718596
  19.2 5.0 %collective-permute-start.2 = (bf16[2,256,256]{2,1,0:T(8,128)(2,1)S(1)}, bf16[2,256,256]{2,1,0:T(8,128)(2,1)S(1)}, u32[]{:S(2)}, u32[]{:S(2)}) collective-permute-start(bf16[2,256,256]{2,1,0:T(8,128)(2,1)S(1)} %get-tuple-element.64), channel_id=1, source_target_pairs={{0,4},{4,8},{8,12},{1,5},{5,9},{9,13},{2,6},{6,10},{10,14},{3,7},{... | collective-permute-start | bytes 786440 | tf_op jit(solution)/shard_map/ppermute | solution.py:578
  20.5 20.4 %collective-permute-start.4 = (bf16[64,16,256]{2,1,0:T(8,128)(2,1)S(1)}, bf16[64,16,256]{2,1,0:T(8,128)(2,1)S(1)}, u32[]{:S(2)}, u32[]{:S(2)}) collective-permute-start(bf16[64,16,256]{2,1,0:T(8,128)(2,1)S(1)} %get-tuple-element.72), channel_id=1, source_target_pairs={{0,12},{4,8},{8,4},{12,0},{1,13},{5,9},{9,5},{13,1},{2,14},{6,10},... | collective-permute-start | bytes 1572872 | tf_op jit(solution)/shard_map/ppermute | solution.py:578
  21.3 9.5 %collective-permute-start.3 = (bf16[3,128,16,256]{3,2,1,0:T(8,128)(2,1)S(1)}, bf16[3,128,16,256]{3,2,1,0:T(8,128)(2,1)S(1)}, u32[]{:S(2)}, u32[]{:S(2)}) collective-permute-start(bf16[3,128,16,256]{3,2,1,0:T(8,128)(2,1)S(1)} %get-tuple-element.69), channel_id=1, source_target_pairs={{0,4},{4,0},{8,12},{12,8},{1,5},{5,1},{9,13},{13,9},{2,6},{6,2},{1... | collective-permute-start | bytes 9437192 | tf_op jit(solution)/shard_map/ppermute | solution.py:578
  34.7 6.2 %collective-permute-start.5 = (f32[128,128]{1,0:T(8,128)S(1)}, f32[128,128]{1,0:T(8,128)S(1)}, u32[]{:S(2)}, u32[]{:S(2)}) collective-permute-start(f32[128,128]{1,0:T(8,128)S(1)} %maxima.1), channel_id=1, source_target_pairs={{8,0},{12,4},{9,1},{13,5},{10,2},{14,6},{11,3},{15,7},{24,16},{28,... | collective-permute-start | bytes 196616 | tf_op jit(solution)/shard_map/ppermute | solution.py:578
  38.2 15.8 %collective-permute-start.6 = (bf16[64,16,256]{2,1,0:T(8,128)(2,1)S(1)}, bf16[64,16,256]{2,1,0:T(8,128)(2,1)S(1)}, u32[]{:S(2)}, u32[]{:S(2)}) collective-permute-start(bf16[64,16,256]{2,1,0:T(8,128)(2,1)S(1)} %get-tuple-element.77), channel_id=1, source_target_pairs={{0,12},{4,8},{8,4},{12,0},{1,13},{5,9},{9,5},{13,1},{2,14},{6,10},... | collective-permute-start | bytes 1572872 | tf_op jit(solution)/shard_map/ppermute | solution.py:578
  41.5 18.7 %collective-permute-start.7 = (bf16[1216,128]{1,0:T(8,128)(2,1)S(1)}, bf16[1216,128]{1,0:T(8,128)(2,1)S(1)}, u32[]{:S(2)}, u32[]{:S(2)}) collective-permute-start(bf16[1216,128]{1,0:T(8,128)(2,1)S(1)} %cross_weights.4), channel_id=1, source_target_pairs={{0,8},{4,12},{1,9},{5,13},{2,10},{6,14},{3,11},{7,15},{16,24},{20,... | collective-permute-start | bytes 933896 | tf_op jit(solution)/shard_map/ppermute | solution.py:578
  52.7 11.8 %collective-permute-start.8 = (bf16[1216,128]{1,0:T(8,128)(2,1)S(1)}, bf16[1216,128]{1,0:T(8,128)(2,1)S(1)}, u32[]{:S(2)}, u32[]{:S(2)}) collective-permute-start(bf16[1216,128]{1,0:T(8,128)(2,1)S(1)} %cross_weights.5), channel_id=1, source_target_pairs={{0,8},{4,12},{1,9},{5,13},{2,10},{6,14},{3,11},{7,15},{16,24},{20,... | collective-permute-start | bytes 933896 | tf_op jit(solution)/shard_map/ppermute | solution.py:578
  55.1 30.1 %collective-permute-start.12 = (bf16[1216,128]{1,0:T(8,128)(2,1)S(1)}, bf16[1216,128]{1,0:T(8,128)(2,1)S(1)}, u32[]{:S(2)}, u32[]{:S(2)}) collective-permute-start(bf16[1216,128]{1,0:T(8,128)(2,1)S(1)} %cross_weights.7), channel_id=1, source_target_pairs={{0,8},{4,12},{1,9},{5,13},{2,10},{6,14},{3,11},{7,15},{16,24},{20,... | collective-permute-start | bytes 933896 | tf_op jit(solution)/shard_map/ppermute | solution.py:578
  56.4 21.4 %collective-permute-start.10 = (bf16[1216,128]{1,0:T(8,128)(2,1)S(1)}, bf16[1216,128]{1,0:T(8,128)(2,1)S(1)}, u32[]{:S(2)}, u32[]{:S(2)}) collective-permute-start(bf16[1216,128]{1,0:T(8,128)(2,1)S(1)} %cross_weights.6), channel_id=1, source_target_pairs={{0,8},{4,12},{1,9},{5,13},{2,10},{6,14},{3,11},{7,15},{16,24},{20,... | collective-permute-start | bytes 933896 | tf_op jit(solution)/shard_map/ppermute | solution.py:578
  63.0 10.1 %collective-permute-start.9 = (bf16[32,16,256]{2,1,0:T(8,128)(2,1)S(1)}, bf16[32,16,256]{2,1,0:T(8,128)(2,1)S(1)}, u32[]{:S(2)}, u32[]{:S(2)}) collective-permute-start(bf16[32,16,256]{2,1,0:T(8,128)(2,1)S(1)} %get-tuple-element.84), channel_id=1, source_target_pairs={{0,4},{4,0},{8,12},{12,8},{1,5},{5,1},{9,13},{13,9},{2,6},{6,2},{1... | collective-permute-start | bytes 786440 | tf_op jit(solution)/shard_map/ppermute | solution.py:578
  67.3 13.3 %collective-permute-start.11 = (bf16[32,16,256]{2,1,0:T(8,128)(2,1)S(1)}, bf16[32,16,256]{2,1,0:T(8,128)(2,1)S(1)}, u32[]{:S(2)}, u32[]{:S(2)}) collective-permute-start(bf16[32,16,256]{2,1,0:T(8,128)(2,1)S(1)} %get-tuple-element.88), channel_id=1, source_target_pairs={{0,4},{4,0},{8,12},{12,8},{1,5},{5,1},{9,13},{13,9},{2,6},{6,2},{1... | collective-permute-start | bytes 786440 | tf_op jit(solution)/shard_map/ppermute | solution.py:578
  82.1 6.0 %collective-permute-start.13 = (bf16[32,16,256]{2,1,0:T(8,128)(2,1)S(1)}, bf16[32,16,256]{2,1,0:T(8,128)(2,1)S(1)}, u32[]{:S(2)}, u32[]{:S(2)}) collective-permute-start(bf16[32,16,256]{2,1,0:T(8,128)(2,1)S(1)} %get-tuple-element.92), channel_id=1, source_target_pairs={{0,4},{4,0},{8,12},{12,8},{1,5},{5,1},{9,13},{13,9},{2,6},{6,2},{1... | collective-permute-start | bytes 786440 | tf_op jit(solution)/shard_map/ppermute | solution.py:578
  88.1 1.6 %collective-permute-start.14 = (bf16[32,16,256]{2,1,0:T(8,128)(2,1)S(1)}, bf16[32,16,256]{2,1,0:T(8,128)(2,1)S(1)}, u32[]{:S(2)}, u32[]{:S(2)}) collective-permute-start(bf16[32,16,256]{2,1,0:T(8,128)(2,1)S(1)} %get-tuple-element.94), channel_id=1, source_target_pairs={{0,4},{4,0},{8,12},{12,8},{1,5},{5,1},{9,13},{13,9},{2,6},{6,2},{1... | collective-permute-start | bytes 786440 | tf_op jit(solution)/shard_map/ppermute | solution.py:578
